TPU v7x, 32 devices: a whole 2x2x4 slice. The times are simulated.
32 devices in a mesh: song: 2 (over x), tm: 8 (over z, y), freq: 2 (over core).
Axes of the slice: x: 2, y: 2, z: 4, core: 2. Of those that a mesh axis runs over, the one named last changes fastest.
Arguments:
- latent: bfloat16 [256, 128, 1024], P(None, 'freq', ('song', 'tm')), parts along dimension 2, as said below
- mel_noisy: float32 [128, 1024], P('freq', ('song', 'tm')), parts along dimension 1, may hold values from -6 to 6
- time_shift: float32 [512], P('song'), parts along dimension 0, may hold values from -3 to 3
- first_gain: float32 [256], replicated, may hold values from 0.5 to 1.5
- first_shift: float32 [256], replicated, may hold values from -3 to 3
- conv_first: bfloat16 [3, 3, 256, 256], replicated, may hold values from -0.125 to 0.125
- second_gain: float32 [256], replicated, may hold values from 0.5 to 1.5
- second_shift: float32 [256], replicated, may hold values from -3 to 3
- conv_second: bfloat16 [3, 3, 256, 256], replicated, may hold values from -0.125 to 0.125
- second_bias: float32 [256], replicated, may hold values from -3 to 3
- out_proj: float32 [256], replicated, may hold values from -0.375 to 0.375
- pre_weight: bfloat16 [1536, 7, 128], P('tm'), may hold values from -0.1875 to 0.1875
- pre_bias: float32 [1536], replicated, may hold values from -3 to 3
- up_weight: bfloat16 [1536, 8, 768], P(None, None, 'freq'), may hold values from -0.109375 to 0.109375
- up_bias: float32 [768], P('freq'), may hold values from -3 to 3
Outputs:
- mel_next: float32 [128, 1024], P('freq', ('song', 'tm')), parts along dimension 1
- vocal: bfloat16 [768, 4096], P('freq', ('song', 'tm')), parts along dimension 1
There are 2 independent parts, one for each index of `song`. A program takes and returns all parts, laid end to end along the dimension named above; an argument that names none is the same for every part. Nothing has to cross between parts.
Inputs may be any that keep to these rules, and one draw needn't show every extreme that they name: `latent`: activations of the block's input, of order one to some tens.
All inputs are finite; a program needn't handle non-finite values.
Results may differ from a plain program's by a relative error of at most 0.0055.
Values may be sent and summed in bfloat16 or wider, within the bound.
No kernel may reach another device: no remote copies, remote signals or barrier semaphores. Data moves between devices by JAX's collectives and lax.ppermute only.
A program may use at most 192 MiB of HBM per device.

v0:
```python
import jax
import jax.numpy as jnp
from jax import lax
from jax.sharding import PartitionSpec as P

GROUPS = 32


EPSILON = 1e-05
STEP_SIZE = 0.25


def padded_2(x, sides, width):
    for axis, dim in sides:
        devices, length = (lax.axis_size(axis), x.shape[dim])
        up = [(i, (i + 1) % devices) for i in range(devices - 1)]
        down = [(j, i) for i, j in up]
        last = lax.slice_in_dim(x, length - width, length, axis=dim)
        first = lax.slice_in_dim(x, 0, width, axis=dim)
        before = lax.ppermute(last, axis, up)
        after = lax.ppermute(first, axis, down)
        x = jnp.concatenate([before, x, after], axis=dim)
    return x


def group_moments(center):
    chans, bins, frames = center.shape
    values = center.astype(jnp.float32).reshape(GROUPS, chans // GROUPS, bins, frames)
    first = jnp.sum(values, axis=(1, 2, 3))
    second = jnp.sum(values * values, axis=(1, 2, 3))
    first, second = lax.psum((first, second), ("tm", "freq"))
    count = float(chans // GROUPS * bins * frames * lax.axis_size("tm") * lax.axis_size("freq"))
    mean = first / count
    var = second / count - mean * mean
    return (mean, lax.rsqrt(var + EPSILON))


def apply_norm(values_in, mean, scale_inv, gain, shift):
    chans, bins, frames = values_in.shape
    values = values_in.astype(jnp.float32).reshape(GROUPS, chans // GROUPS, bins, frames)
    scaled = (values - mean[:, None, None, None]) * scale_inv[:, None, None, None]
    scaled = scaled.reshape(chans, bins, frames) * gain[:, None, None] + shift[:, None, None]
    return jax.nn.silu(scaled)


def norm_silu(values_in, gain, shift):
    mean, scale_inv = group_moments(values_in)
    return apply_norm(values_in, mean, scale_inv, gain, shift).astype(jnp.bfloat16)


def conv_valid(padded, weight, bins, frames):
    total = jnp.zeros((weight.shape[3], bins, frames), jnp.float32)
    for i in range(3):
        for j in range(3):
            total = total + jnp.einsum(
                "io,ift->oft",
                weight[i, j],
                padded[:, i : i + bins, j : j + frames],
                preferred_element_type=jnp.float32,
            )
    return total


def conv_three(active, weight):
    bins, frames = (active.shape[1], active.shape[2])
    padded = padded_2(active, (("tm", 2), ("freq", 1)), 1)
    return conv_valid(padded, weight, bins, frames)


def up_tap(up_weight, k, feats):
    return jnp.einsum("io,it->ot", up_weight[:, k, :], feats, preferred_element_type=jnp.float32)


def shards(
    latent,
    mel_noisy,
    time_shift,
    first_gain,
    first_shift,
    conv_first,
    second_gain,
    second_shift,
    conv_second,
    second_bias,
    out_proj,
    pre_weight,
    pre_bias,
    up_weight,
    up_bias,
):
    active = norm_silu(latent, first_gain, first_shift)
    first_out = (conv_three(active, conv_first) + time_shift[:, None, None]).astype(jnp.bfloat16)
    second_in = norm_silu(first_out, second_gain, second_shift)
    second_conv = conv_three(second_in, conv_second)
    hidden = latent.astype(jnp.float32) + second_conv + second_bias[:, None, None]
    velocity = jnp.sum(out_proj[:, None, None] * hidden, axis=0)
    mel_next = mel_noisy + STEP_SIZE * velocity
    mel_in = mel_next.astype(jnp.bfloat16)
    mel_full = lax.all_gather(mel_in, "freq", axis=0, tiled=True)
    frames = mel_full.shape[1]
    taps = pre_weight.shape[1]
    extended = padded_2(mel_full, (("tm", 1),), 4)
    piece = lax.all_gather(pre_weight, "tm", axis=0, tiled=True)
    total = jnp.zeros((piece.shape[0], frames + 2), jnp.float32)
    for k in range(taps):
        total = total + jnp.dot(
            piece[:, k, :], extended[:, k : k + frames + 2], preferred_element_type=jnp.float32
        )
    position = lax.axis_index("tm") * frames - 1 + jnp.arange(frames + 2, dtype=jnp.int32)
    valid = (position >= 0) & (position < frames * lax.axis_size("tm"))
    features = jnp.where(valid[None, :], total + pre_bias[:, None], 0.0).astype(jnp.bfloat16)
    middle = features[:, 1 : frames + 1]
    before = features[:, 0:frames]
    after = features[:, 2 : frames + 2]
    phases = []
    for p in range(4):
        term = up_tap(up_weight, p + 2, middle)
        if p <= 1:
            term = term + up_tap(up_weight, p + 6, before)
        else:
            term = term + up_tap(up_weight, p - 2, after)
        phases.append(term)
    stacked = jnp.stack(phases, axis=2).reshape(up_weight.shape[2], 4 * frames)
    vocal = (stacked + up_bias[:, None]).astype(jnp.bfloat16)
    return (mel_next, vocal)


def solution(mesh):
    in_specs = (
        P(None, "freq", ("song", "tm")),
        P("freq", ("song", "tm")),
        P("song"),
        P(),
        P(),
        P(),
        P(),
        P(),
        P(),
        P(),
        P(),
        P("tm", None, None),
        P(),
        P(None, None, "freq"),
        P("freq"),
    )
    out_specs = (P("freq", ("song", "tm")), P("freq", ("song", "tm")))
    return jax.shard_map(shards, mesh=mesh, in_specs=in_specs, out_specs=out_specs, check_vma=False)
```

profile of v0, /device:TPU:0, one launch (start us, length us, event | category | flops | bytes accessed | tf_op | source)
XLA Modules:
  0.0 244.6 jit_solution(2898610104928867192)
XLA Ops:
  7.2 2.2 convert_reduce_fusion
  9.8 35.0 %all-reduce.1 = (f32[32]{0:T(128)S(1)}, f32[32]{0:T(128)S(1)}) all-reduce(f32[32]{0:T(128)S(1)} %reduce_sum.62, f32[32]{0:T(128)S(1)} %reduce_sum.59), channel_id=1, replica_groups=mesh['song'=2,'tm'=8,'freq'=2] {'tm','freq'}, use_global_device_ids=true, to_apply=%region_5.6 | all-reduce | flops 64 | bytes 512 | tf_op jit(solution)/shard_map/psum | solution.py:31
  45.1 3.0 %fusion.19 = bf16[256,64,64]{0,2,1:T(8,128)(2,1)S(1)} fusion(bf16[256,64,64]{0,2,1:T(8,128)(2,1)} %param.15, f32[256]{0:T(256)} %param.19, f32[256]{0:T(256)} %param.18, f32[256]{0:T(256)S(1)} %mul.84, f32[256]{0:T(256)S(1)} %sub.36), kind=kLoop, calls=%fused_computation.26 | loop fusion | flops 10485760 | bytes 4198400 | tf_op jit(solution)/shard_map/convert_element_type | solution.py:48
  48.3 1.3 collective-permute-start
  49.6 1.3 collective-permute-start.1
  50.9 44.2 %fusion.172 = (bf16[1536,1,384]{2,1,0:T(2,128)(2,1)}, bf16[1536,1,384]{2,1,0:T(2,128)(2,1)}, bf16[1536,1,384]{2,1,0:T(2,128)(2,1)}, bf16[1536,1,384]{2,1,0:T(2,1...) fusion(bf16[1536,8,384]{2,1,0:T(8,128)(2,1)} %param.28), kind=kLoop, calls=%fused_computation.218 | loop fusion | bytes 18874368 | tf_op jit(solution)/shard_map/slice | solution.py:71
  95.1 2.6 %fusion.109 = f32[64,64,256]{2,1,0:T(8,128)} fusion(bf16[256,64,64]{0,2,1:T(8,128)(2,1)S(1)} %fusion.19, bf16[3,3,256,256]{3,2,1,0:T(8,128)(2,1)S(1)} %copy-done.10), kind=kOutput, calls=%fused_computation.139 | convolution fusion | flops 536870912 | bytes 6422528 | tf_op jit(solution)/shard_map/io,ift->oft/dot_general | solution.py:55
  97.8 1.3 collective-permute-start.2
  99.1 1.5 collective-permute-start.3
  100.5 2.7 %fusion.59 = f32[64,64,256]{2,1,0:T(8,128)} fusion(bf16[256,64,1]{0,2,1:T(2,128)(2,1)S(1)} %collective-permute-done.1, bf16[256,64,64]{0,2,1:T(8,128)(2,1)S(1)} %fusion.19, bf16[3,3,256,256]{3,2,1,0:T(8,128)(2,1)S(1)} %copy-done.10), kind=kOutput, calls=%fused_computation.71 | convolution fusion | flops 541065216 | bytes 6488064 | tf_op jit(solution)/shard_map/io,ift->oft/dot_general | solution.py:55
  103.2 2.7 %fusion.61 = f32[64,64,256]{2,1,0:T(8,128)} fusion(bf16[256,64,64]{0,2,1:T(8,128)(2,1)S(1)} %fusion.19, bf16[256,64,1]{0,2,1:T(2,128)(2,1)S(1)} %collective-permute-done, bf16[3,3,256,256]{3,2,1,0:T(8,128)(2,1)S(1)} %copy-done.10), kind=kOutput, calls=%fused_computation.74 | convolution fusion | flops 541065216 | bytes 6488064 | tf_op jit(solution)/shard_map/io,ift->oft/dot_general | solution.py:55
  105.9 2.8 %maximum_maximum_fusion = (bf16[256,65,66]{0,2,1:T(8,128)(2,1)S(1)}, bf16[256,65,66]{0,2,1:T(8,128)(2,1)S(1)}) fusion(bf16[256,64,1]{0,2,1:T(2,128)(2,1)S(1)} %collective-permute-done.1, bf16[256,64,64]{0,2,1:T(8,128)(2,1)S(1)} %fusion.19, bf16[256,64,1]{0,2,1:T(2,128)(2,1)S(1)} %collective-permute-done, bf16[256,1,66]{0,2,1:T(8,128)(2,1)S(1)} %collective-permute-done.2, ...), kind=kLoop, calls=%fused_computation.32 | loop fusion | flops 17571840 | bytes 6623232 | tf_op jit(solution)/shard_map/concatenate | solution.py:22
  108.7 2.7 %fusion.55 = f32[64,64,256]{2,1,0:T(8,128)} fusion(bf16[256,65,66]{0,2,1:T(8,128)(2,1)S(1)} %get-tuple-element.27, bf16[3,3,256,256]{3,2,1,0:T(8,128)(2,1)S(1)} %copy-done.10), kind=kOutput, calls=%fused_computation.66 | convolution fusion | flops 536870912 | bytes 6422528 | tf_op jit(solution)/shard_map/io,ift->oft/dot_general | solution.py:55
  111.4 2.7 %fusion.57 = f32[64,64,256]{2,1,0:T(8,128)} fusion(bf16[256,65,66]{0,2,1:T(8,128)(2,1)S(1)} %get-tuple-element.27, bf16[3,3,256,256]{3,2,1,0:T(8,128)(2,1)S(1)} %copy-done.10), kind=kOutput, calls=%fused_computation.68 | convolution fusion | flops 536870912 | bytes 6422528 | tf_op jit(solution)/shard_map/io,ift->oft/dot_general | solution.py:55
  114.1 2.7 %fusion.63 = f32[64,64,256]{2,1,0:T(8,128)} fusion(bf16[256,65,66]{0,2,1:T(8,128)(2,1)S(1)} %get-tuple-element.26, bf16[3,3,256,256]{3,2,1,0:T(8,128)(2,1)S(1)} %copy-done.10), kind=kOutput, calls=%fused_computation.76 | convolution fusion | flops 536870912 | bytes 6422528 | tf_op jit(solution)/shard_map/io,ift->oft/dot_general | solution.py:55
  116.8 2.7 %fusion.65 = f32[64,64,256]{2,1,0:T(8,128)} fusion(bf16[256,65,66]{0,2,1:T(8,128)(2,1)S(1)} %get-tuple-element.26, bf16[3,3,256,256]{3,2,1,0:T(8,128)(2,1)S(1)} %copy-done.10), kind=kOutput, calls=%fused_computation.78 | convolution fusion | flops 536870912 | bytes 6422528 | tf_op jit(solution)/shard_map/io,ift->oft/dot_general | solution.py:55
  119.4 2.8 %fusion.67 = f32[64,64,256]{2,1,0:T(8,128)} fusion(bf16[256,65,66]{0,2,1:T(8,128)(2,1)S(1)} %get-tuple-element.26, bf16[3,3,256,256]{3,2,1,0:T(8,128)(2,1)S(1)} %copy-done.10), kind=kOutput, calls=%fused_computation.80 | convolution fusion | flops 536870912 | bytes 6422528 | tf_op jit(solution)/shard_map/io,ift->oft/dot_general | solution.py:55
  122.2 0.8 copy-done.1
  123.0 10.8 %convert_reduce_fusion.1 = (f32[256]{0:T(256)S(1)}, f32[256]{0:T(256)S(1)}, bf16[64,64,256]{2,1,0:T(8,128)(2,1)S(1)}) fusion(f32[256]{0:T(256)S(1)} %copy-done.14, bf16[3,3,256,256]{3,2,1,0:T(8,128)(2,1)} %param.20, bf16[256,65,66]{0,2,1:T(8,128)(2,1)S(1)} %get-tuple-element.27, f32[64,64,256]{2,1,0:T(8,128)} %fusion.55, f32[64,64,256]{2,1,0:T(8,128)} %fusion.57, ...), kind=kOutput, calls=%fused_computation.5 | convolution fusion | flops 551550464 | bytes 37882880 | tf_op jit(solution)/shard_map/io,ift->oft/dot_general | solution.py:55
  134.2 33.4 %all-reduce = (f32[32]{0:T(128)S(1)}, f32[32]{0:T(128)S(1)}) all-reduce(f32[32]{0:T(128)S(1)} %reduce_sum.84, f32[32]{0:T(128)S(1)} %reduce_sum.81), channel_id=1, replica_groups=mesh['song'=2,'tm'=8,'freq'=2] {'tm','freq'}, use_global_device_ids=true, to_apply=%region_11.12 | all-reduce | flops 64 | bytes 512 | tf_op jit(solution)/shard_map/psum | solution.py:31
  168.0 1.4 fusion.10
  169.5 1.3 collective-permute-start.4
  170.8 1.4 collective-permute-start.5
  172.3 1.6 fusion.99
  173.9 3.2 %collective-permute-done.5 = bf16[256,64,1]{0,2,1:T(2,128)(2,1)S(1)} collective-permute-done((bf16[256,64,1]{0,2,1:T(2,128)(2,1)S(1)}, bf16[256,64,1]{0,2,1:T(2,128)(2,1)S(1)}, u32[]{:S(2)}, u32[]{:S(2)}) %collective-permute-start.5) | collective-permute-done | bytes 32800 | tf_op jit(solution)/shard_map/ppermute | solution.py:21
  177.2 1.3 collective-permute-start.6
  178.5 1.5 collective-permute-start.7
  180.0 2.7 %fusion.43 = f32[64,64,256]{2,1,0:T(8,128)} fusion(bf16[256,64,64]{0,2,1:T(8,128)(2,1)S(1)} %fusion.10, bf16[256,64,1]{0,2,1:T(2,128)(2,1)S(1)} %collective-permute-done.4, bf16[3,3,256,256]{3,2,1,0:T(8,128)(2,1)S(1)} %copy-done.11), kind=kOutput, calls=%fused_computation.56 | convolution fusion | flops 541065216 | bytes 6488064 | tf_op jit(solution)/shard_map/io,ift->oft/dot_general | solution.py:55
  182.6 2.7 %fusion.41 = f32[64,64,256]{2,1,0:T(8,128)} fusion(bf16[256,64,1]{0,2,1:T(2,128)(2,1)S(1)} %collective-permute-done.5, bf16[256,64,64]{0,2,1:T(8,128)(2,1)S(1)} %fusion.10, bf16[3,3,256,256]{3,2,1,0:T(8,128)(2,1)S(1)} %copy-done.11), kind=kOutput, calls=%fused_computation.53 | convolution fusion | flops 541065216 | bytes 6488064 | tf_op jit(solution)/shard_map/io,ift->oft/dot_general | solution.py:55
  185.3 2.8 %maximum_maximum_fusion.1 = (bf16[256,65,66]{0,2,1:T(8,128)(2,1)S(1)}, bf16[256,65,66]{0,2,1:T(8,128)(2,1)S(1)}) fusion(bf16[256,64,1]{0,2,1:T(2,128)(2,1)S(1)} %collective-permute-done.5, bf16[256,64,64]{0,2,1:T(8,128)(2,1)S(1)} %fusion.10, bf16[256,64,1]{0,2,1:T(2,128)(2,1)S(1)} %collective-permute-done.4, ...), kind=kLoop, calls=%fused_computation.34 | loop fusion | flops 17571840 | bytes 6623232 | tf_op jit(solution)/shard_map/concatenate | solution.py:22
  188.2 2.7 %fusion.37 = f32[64,64,256]{2,1,0:T(8,128)} fusion(bf16[256,65,66]{0,2,1:T(8,128)(2,1)S(1)} %get-tuple-element.23, bf16[3,3,256,256]{3,2,1,0:T(8,128)(2,1)S(1)} %copy-done.11), kind=kOutput, calls=%fused_computation.48 | convolution fusion | flops 536870912 | bytes 6422528 | tf_op jit(solution)/shard_map/io,ift->oft/dot_general | solution.py:55
  190.9 2.7 %fusion.39 = f32[64,64,256]{2,1,0:T(8,128)} fusion(bf16[256,65,66]{0,2,1:T(8,128)(2,1)S(1)} %get-tuple-element.23, bf16[3,3,256,256]{3,2,1,0:T(8,128)(2,1)S(1)} %copy-done.11), kind=kOutput, calls=%fused_computation.50 | convolution fusion | flops 536870912 | bytes 6422528 | tf_op jit(solution)/shard_map/io,ift->oft/dot_general | solution.py:55
  193.5 2.7 %fusion.45 = f32[64,64,256]{2,1,0:T(8,128)} fusion(bf16[256,65,66]{0,2,1:T(8,128)(2,1)S(1)} %get-tuple-element.22, bf16[3,3,256,256]{3,2,1,0:T(8,128)(2,1)S(1)} %copy-done.11), kind=kOutput, calls=%fused_computation.58 | convolution fusion | flops 536870912 | bytes 6422528 | tf_op jit(solution)/shard_map/io,ift->oft/dot_general | solution.py:55
  196.2 2.7 %fusion.47 = f32[64,64,256]{2,1,0:T(8,128)} fusion(bf16[256,65,66]{0,2,1:T(8,128)(2,1)S(1)} %get-tuple-element.22, bf16[3,3,256,256]{3,2,1,0:T(8,128)(2,1)S(1)} %copy-done.11), kind=kOutput, calls=%fused_computation.60 | convolution fusion | flops 536870912 | bytes 6422528 | tf_op jit(solution)/shard_map/io,ift->oft/dot_general | solution.py:55
  198.9 2.7 %fusion.49 = f32[64,64,256]{2,1,0:T(8,128)} fusion(bf16[256,65,66]{0,2,1:T(8,128)(2,1)S(1)} %get-tuple-element.22, bf16[3,3,256,256]{3,2,1,0:T(8,128)(2,1)S(1)} %copy-done.11), kind=kOutput, calls=%fused_computation.62 | convolution fusion | flops 536870912 | bytes 6422528 | tf_op jit(solution)/shard_map/io,ift->oft/dot_general | solution.py:55
  201.6 10.9 %fusion.23 = f32[64,64]{1,0:T(8,128)S(1)} fusion(bf16[256,64,64]{0,2,1:T(8,128)(2,1)S(1)} %copy-done, f32[64,64,256]{2,1,0:T(8,128)} %fusion.37, f32[64,64,256]{2,1,0:T(8,128)} %fusion.39, f32[64,64,256]{2,1,0:T(8,128)} %fusion.41, f32[64,64,256]{2,1,0:T(8,128)S(1)} %fusion.99, f32[64,64,256]{2,1,0:T(8,128)} %fusion.43, f32[64,64,256]{2,1,0:T(8,128)} %fusion.45, ...), kind=kOutput, calls=%fused_computation.30 | convolution fusion | flops 550498304 | bytes 37898240 | tf_op jit(solution)/shard_map/io,ift->oft/dot_general | solution.py:55
  212.4 1.4 fusion.171
  213.8 2.6 %all_gather.6 = bf16[128,64]{1,0:T(8,128)(2,1)S(1)} all-gather(bf16[64,64]{1,0:T(8,128)(2,1)S(1)} %get-tuple-element.12), channel_id=1, replica_groups=mesh['song'=2,'tm'=8,'freq'=2] {'freq'}, dimensions={0}, use_global_device_ids=true | all-gather | bytes 24576 | tf_op jit(solution)/shard_map/all_gather | solution.py:99
  216.4 1.6 collective-permute-start.8
  218.0 1.3 collective-permute-start.9
  219.3 0.3 collective-permute-done.8
  219.6 1.4 fusion.90
  221.0 1.4 fusion.89
  222.5 1.4 collective-permute-done.9
  223.8 1.6 fusion.88
  225.4 1.4 fusion.87
  226.9 1.6 fusion.86
  228.4 1.4 fusion.85
  229.9 1.6 fusion.32
  231.5 0.3 fusion.75
  231.8 0.3 fusion.73
  232.2 0.3 fusion.71
  232.5 0.7 copy-done.6
  233.2 0.3 fusion.69
  233.5 0.4 copy-done.5
  233.9 0.3 fusion.78
  234.3 0.5 copy-done.4
  234.7 0.3 fusion.80
  235.1 0.4 copy-done.3
  235.4 0.3 fusion.82
  235.8 0.3 copy-done.2
  236.1 0.3 fusion.84
  236.5 0.3 copy.25
  236.9 0.8 copy.26
  (65 shorter events, 2.2 us)
Async XLA Ops:
  7.2 212.4 %all-gather.2.cloned.1.call-start = ((), (), s32[]{:S(2)}) async-start(), calls=%async_computation | async-start | bytes 3096576 | tf_op jit(solution)/shard_map/all_gather | solution.py:103
  48.3 49.5 %collective-permute-start = (bf16[256,64,1]{0,2,1:T(2,128)(2,1)S(1)}, bf16[256,64,1]{0,2,1:T(2,128)(2,1)S(1)}, u32[]{:S(2)}, u32[]{:S(2)}) collective-permute-start(bf16[256,64,1]{0,2,1:T(2,128)(2,1)S(1)} %get-tuple-element.32), channel_id=1, source_target_pairs={{0,2},{2,4},{4,6},{6,8},{8,10},{10,12},{12,14},{1,3},{3,5},{5,7},{... | collective-permute-start | bytes 98312 | tf_op jit(solution)/shard_map/ppermute | solution.py:20
  49.6 48.2 %collective-permute-start.1 = (bf16[256,64,1]{0,2,1:T(2,128)(2,1)S(1)}, bf16[256,64,1]{0,2,1:T(2,128)(2,1)S(1)}, u32[]{:S(2)}, u32[]{:S(2)}) collective-permute-start(bf16[256,64,1]{0,2,1:T(2,128)(2,1)S(1)} %get-tuple-element.33), channel_id=1, source_target_pairs={{2,0},{4,2},{6,4},{8,6},{10,8},{12,10},{14,12},{3,1},{5,3},{7,5},{... | collective-permute-start | bytes 98312 | tf_op jit(solution)/shard_map/ppermute | solution.py:21
  50.9 44.2 %copy-start.10 = (bf16[3,3,256,256]{3,2,1,0:T(8,128)(2,1)S(1)}, bf16[3,3,256,256]{3,2,1,0:T(8,128)(2,1)}, u32[]{:S(2)}) copy-start(bf16[3,3,256,256]{3,2,1,0:T(8,128)(2,1)} %param.20) | copy-start | bytes 3538948
  97.8 8.1 %collective-permute-start.2 = (bf16[256,1,66]{0,2,1:T(8,128)(2,1)S(1)}, bf16[256,1,66]{0,2,1:T(8,128)(2,1)S(1)}, u32[]{:S(2)}, u32[]{:S(2)}) collective-permute-start(bf16[256,1,66]{0,2,1:T(8,128)(2,1)S(1)} %get-tuple-element.28), channel_id=1, source_target_pairs={{0,1},{2,3},{4,5},{6,7},{8,9},{10,11},{12,13},{14,15},{16,17},{18,... | collective-permute-start | bytes 101384 | tf_op jit(solution)/shard_map/ppermute | solution.py:20
  99.1 6.8 %collective-permute-start.3 = (bf16[256,1,66]{0,2,1:T(8,128)(2,1)S(1)}, bf16[256,1,66]{0,2,1:T(8,128)(2,1)S(1)}, u32[]{:S(2)}, u32[]{:S(2)}) collective-permute-start(bf16[256,1,66]{0,2,1:T(8,128)(2,1)S(1)} %get-tuple-element.29), channel_id=1, source_target_pairs={{1,0},{3,2},{5,4},{7,6},{9,8},{11,10},{13,12},{15,14},{17,16},{19,... | collective-permute-start | bytes 101384 | tf_op jit(solution)/shard_map/ppermute | solution.py:21
  119.4 3.5 %copy-start.1 = (f32[64,64,256]{2,1,0:T(8,128)S(1)}, f32[64,64,256]{2,1,0:T(8,128)}, u32[]{:S(2)}) copy-start(f32[64,64,256]{2,1,0:T(8,128)} %fusion.109) | copy-start | bytes 12582916
  119.4 3.5 %copy-start.14 = (f32[256]{0:T(256)S(1)}, f32[256]{0:T(256)}, u32[]{:S(2)}) copy-start(f32[256]{0:T(256)} %param.17) | copy-start | bytes 3076
  123.0 45.0 %copy-start.15 = (f32[256]{0:T(256)S(1)}, f32[256]{0:T(256)}, u32[]{:S(2)}) copy-start(f32[256]{0:T(256)} %param.22) | copy-start | bytes 3076
  123.0 45.0 %copy-start.16 = (f32[256]{0:T(256)S(1)}, f32[256]{0:T(256)}, u32[]{:S(2)}) copy-start(f32[256]{0:T(256)} %param.21) | copy-start | bytes 3076
  169.5 4.4 %collective-permute-start.4 = (bf16[256,64,1]{0,2,1:T(2,128)(2,1)S(1)}, bf16[256,64,1]{0,2,1:T(2,128)(2,1)S(1)}, u32[]{:S(2)}, u32[]{:S(2)}) collective-permute-start(bf16[256,64,1]{0,2,1:T(2,128)(2,1)S(1)} %get-tuple-element.30), channel_id=1, source_target_pairs={{0,2},{2,4},{4,6},{6,8},{8,10},{10,12},{12,14},{1,3},{3,5},{5,7},{... | collective-permute-start | bytes 98312 | tf_op jit(solution)/shard_map/ppermute | solution.py:20
  170.8 9.2 %copy-start.11 = (bf16[3,3,256,256]{3,2,1,0:T(8,128)(2,1)S(1)}, bf16[3,3,256,256]{3,2,1,0:T(8,128)(2,1)}, u32[]{:S(2)}) copy-start(bf16[3,3,256,256]{3,2,1,0:T(8,128)(2,1)} %param.23) | copy-start | bytes 3538948
  170.8 6.3 %collective-permute-start.5 = (bf16[256,64,1]{0,2,1:T(2,128)(2,1)S(1)}, bf16[256,64,1]{0,2,1:T(2,128)(2,1)S(1)}, u32[]{:S(2)}, u32[]{:S(2)}) collective-permute-start(bf16[256,64,1]{0,2,1:T(2,128)(2,1)S(1)} %get-tuple-element.31), channel_id=1, source_target_pairs={{2,0},{4,2},{6,4},{8,6},{10,8},{12,10},{14,12},{3,1},{5,3},{7,5},{... | collective-permute-start | bytes 98312 | tf_op jit(solution)/shard_map/ppermute | solution.py:21
  177.2 8.2 %collective-permute-start.6 = (bf16[256,1,66]{0,2,1:T(8,128)(2,1)S(1)}, bf16[256,1,66]{0,2,1:T(8,128)(2,1)S(1)}, u32[]{:S(2)}, u32[]{:S(2)}) collective-permute-start(bf16[256,1,66]{0,2,1:T(8,128)(2,1)S(1)} %get-tuple-element.24), channel_id=1, source_target_pairs={{0,1},{2,3},{4,5},{6,7},{8,9},{10,11},{12,13},{14,15},{16,17},{18,... | collective-permute-start | bytes 101384 | tf_op jit(solution)/shard_map/ppermute | solution.py:20
  178.5 6.9 %collective-permute-start.7 = (bf16[256,1,66]{0,2,1:T(8,128)(2,1)S(1)}, bf16[256,1,66]{0,2,1:T(8,128)(2,1)S(1)}, u32[]{:S(2)}, u32[]{:S(2)}) collective-permute-start(bf16[256,1,66]{0,2,1:T(8,128)(2,1)S(1)} %get-tuple-element.25), channel_id=1, source_target_pairs={{1,0},{3,2},{5,4},{7,6},{9,8},{11,10},{13,12},{15,14},{17,16},{19,... | collective-permute-start | bytes 101384 | tf_op jit(solution)/shard_map/ppermute | solution.py:21
  198.9 2.7 %copy-start = (bf16[256,64,64]{0,2,1:T(8,128)(2,1)S(1)}, bf16[256,64,64]{0,2,1:T(8,128)(2,1)}, u32[]{:S(2)}) copy-start(bf16[256,64,64]{0,2,1:T(8,128)(2,1)} %param.15) | copy-start | bytes 6291460
  216.4 3.1 %collective-permute-start.8 = (bf16[128,4]{1,0:T(8,128)(2,1)S(1)}, bf16[128,4]{1,0:T(8,128)(2,1)S(1)}, u32[]{:S(2)}, u32[]{:S(2)}) collective-permute-start(bf16[128,4]{1,0:T(8,128)(2,1)S(1)} %get-tuple-element.34), channel_id=1, source_target_pairs={{0,2},{2,4},{4,6},{6,8},{8,10},{10,12},{12,14},{1,3},{3,5},{5,7},{... | collective-permute-start | bytes 3080 | tf_op jit(solution)/shard_map/ppermute | solution.py:20
  218.0 5.8 %collective-permute-start.9 = (bf16[128,4]{1,0:T(8,128)(2,1)S(1)}, bf16[128,4]{1,0:T(8,128)(2,1)S(1)}, u32[]{:S(2)}, u32[]{:S(2)}) collective-permute-start(bf16[128,4]{1,0:T(8,128)(2,1)S(1)} %get-tuple-element.35), channel_id=1, source_target_pairs={{2,0},{4,2},{6,4},{8,6},{10,8},{12,10},{14,12},{3,1},{5,3},{7,5},{... | collective-permute-start | bytes 3080 | tf_op jit(solution)/shard_map/ppermute | solution.py:21
  221.0 8.8 %copy-start.12 = (f32[1536]{0:T(1024)S(1)}, f32[1536]{0:T(1024)}, u32[]{:S(2)}) copy-start(f32[1536]{0:T(1024)} %param.27) | copy-start | bytes 18436
  223.8 7.6 %copy-start.9 = (bf16[1536,1,384]{2,1,0:T(2,128)(2,1)S(1)}, bf16[1536,1,384]{2,1,0:T(2,128)(2,1)}, u32[]{:S(2)}) copy-start(bf16[1536,1,384]{2,1,0:T(2,128)(2,1)} %get-tuple-element.20) | copy-start | bytes 3538948
  226.8 5.0 %copy-start.8 = (bf16[1536,1,384]{2,1,0:T(2,128)(2,1)S(1)}, bf16[1536,1,384]{2,1,0:T(2,128)(2,1)}, u32[]{:S(2)}) copy-start(bf16[1536,1,384]{2,1,0:T(2,128)(2,1)} %get-tuple-element.18) | copy-start | bytes 3538948
  229.9 2.3 copy-start.7
  231.5 1.7 copy-start.6
  231.8 2.1 copy-start.5
  232.2 2.6 %copy-start.4 = (bf16[1536,1,384]{2,1,0:T(2,128)(2,1)S(1)}, bf16[1536,1,384]{2,1,0:T(2,128)(2,1)}, u32[]{:S(2)}) copy-start(bf16[1536,1,384]{2,1,0:T(2,128)(2,1)} %get-tuple-element.19) | copy-start | bytes 3538948
  233.2 2.3 copy-start.3
  233.9 2.2 copy-start.2
  235.8 1.1 copy-start.13
Sparse Core Ops, SparseCore 0:
  51.0 55.3 all-gather.1
where the time goes:
time: 245 us
  matrix products  76.5 us (31%)
  blocking collectives  70.9 us (29%)
  local copies, waits for them, and re-layouts  49.7 us (20%)
  between operations  14.5 us (6%)
  other arithmetic  14.3 us (6%)
  starting transfers between devices  13.8 us (6%)
  waiting for transfers between devices  4.92 us (2%)
    psum x2, blocking collectives, group_moments(): first, second = lax.psum((first, second), ('tm', 'freq'))  68.3 us
    dot_general x18, matrix products, conv_valid(): jnp.einsum('io,ift->oft', weight[i, j], padded[:, i:i + bins, j:j + frame...  63.5 us
    slice x1, local copies, waits for them, and re-layouts, up_tap(): up_weight[:, k, :]  44.2 us
    dot_general x7, matrix products, shards(): jnp.dot(piece[:, k, :], extended[:, k:k + frames + 2], preferred_element_...  10.4 us
    ppermute x5, starting transfers between devices, padded_2(): after = lax.ppermute(first, axis, down)  6.99 us
    ppermute x5, starting transfers between devices, padded_2(): before = lax.ppermute(last, axis, up)  6.73 us
    concatenate x2, other arithmetic, padded_2(): x = jnp.concatenate([before, x, after], axis=dim)  5.65 us
  transfers between devices with their start and end apart: 11, of which 3 were waited for; matrix products, arithmetic and copies ran while one was open for 49% of the time, Pallas kernels for 0%

commit v1 on v0

v1 whole, which is shorter than its diff:
```python
import functools

import jax
import jax.numpy as jnp
from jax import lax
from jax.experimental import pallas as pl
from jax.experimental.pallas import tpu as pltpu
from jax.sharding import PartitionSpec as P

GROUPS = 32
EPSILON = 1e-05
STEP_SIZE = 0.25
EDGE = 8
F32 = jnp.float32
BF16 = jnp.bfloat16
VMEM = pl.BlockSpec(memory_space=pltpu.VMEM)
SMEM = pl.BlockSpec(memory_space=pltpu.SMEM)


def nt(a, b):
    return lax.dot_general(a, b, (((1,), (1,)), ((), ())), preferred_element_type=F32)


def split3(x):
    hi = x.astype(BF16)
    rest = x - hi.astype(F32)
    mid = rest.astype(BF16)
    low = (rest - mid.astype(F32)).astype(BF16)
    return hi, mid, low


def norm_terms(stats, gain, count):
    chans = stats.shape[1] // 2
    total = jnp.sum(stats, axis=0, keepdims=True)
    size = chans // GROUPS
    rows = lax.broadcasted_iota(jnp.int32, (chans, chans), 0) // size
    cols = lax.broadcasted_iota(jnp.int32, (chans, chans), 1) // size
    same = jnp.where(rows == cols, 1.0, 0.0).astype(F32)
    both = jnp.concatenate([total[:, :chans], total[:, chans:]], axis=0)
    both = jnp.concatenate([both, jnp.zeros((6, chans), F32)], axis=0)
    groups = lax.dot_general(
        both, same, (((1,), (0,)), ((), ())), precision=lax.Precision.HIGHEST, preferred_element_type=F32
    )
    mean = groups[0:1] / count
    var = groups[1:2] / count - mean * mean
    return mean, lax.rsqrt(var + EPSILON) * gain


def half_silu(values, mean, scale, shift):
    half = (values - mean) * (scale * 0.5) + shift * 0.5
    return half + half * jnp.tanh(half)


def conv_kernel(bins, frames, rows, count, info, stats, gain, shift, tshift, own, left, right, top, bottom,
                weight, proj, out, moments, base, act):
    chans = own.shape[-1]
    width = frames + 2 * EDGE
    tm, tms, fq, fqs = info[0], info[1], info[2], info[3]
    mean, scale = norm_terms(stats[...], gain[...], count)
    shift_v = shift[...]
    place = lax.broadcasted_iota(jnp.int32, (width, 1), 0) - EDGE + tm * frames
    inside = jnp.where((place >= 0) & (place < frames * tms), 1.0, 0.0).astype(F32)
    inside = jnp.broadcast_to(inside, (width, chans))

    def put(row, middle, bin_ok):
        l32, m32, r32 = left[row].astype(F32), middle.astype(F32), right[row].astype(F32)
        raw = jnp.concatenate([l32, m32, r32], axis=0)
        val = half_silu(raw, mean, scale, shift_v)
        keep = inside > 0.0 if bin_ok is None else (inside * bin_ok) > 0.0
        val = jnp.where(keep, val, 0.0)
        act[row, :, 0:chans] = pltpu.roll(val, 1, 0).astype(BF16)
        act[row, :, chans : 2 * chans] = val.astype(BF16)
        act[row, :, 2 * chans : 3 * chans] = pltpu.roll(val, width - 1, 0).astype(BF16)
        return raw

    has_top = jnp.where(fq > 0, 1.0, 0.0).astype(F32)
    has_bottom = jnp.where(fq < fqs - 1, 1.0, 0.0).astype(F32)

    def put_own(i):
        raw = put(i + 2, own[i], None)
        parts = nt(proj[...], raw.astype(BF16))
        base[i] = parts[0:8] + parts[8:16] + parts[16:24]

    put(0, top[0], has_top)
    put(1, top[1], has_top)
    for i in range(rows):
        put_own(i)
    put(bins + 2, bottom[0], has_bottom)
    put(bins + 3, bottom[1], has_bottom)

    blocks = (bins + 2) // rows

    def matmul(b, acc_s, acc_q):
        first = b * rows
        lhs = jnp.concatenate([act[pl.ds(first + i, rows)] for i in range(3)], axis=-1)
        lhs = lhs.reshape(rows * width, 9 * chans)
        res = jnp.dot(lhs, weight[...], preferred_element_type=F32) + tshift[...]
        res = res.reshape(rows, width, chans).astype(BF16)
        out[pl.ds(first, rows)] = res
        for r in range(rows):
            line = first + r
            ok = jnp.where((line >= 1) & (line <= bins), 1.0, 0.0).astype(F32)
            vals = res[r].astype(F32)[EDGE : EDGE + frames] * ok
            vals = vals.reshape(frames // 8, 8, chans)
            acc_s = acc_s + jnp.sum(vals, axis=0)
            acc_q = acc_q + jnp.sum(vals * vals, axis=0)
        return acc_s, acc_q

    def step(b, carry):
        for r in range(rows):
            i = b * rows + rows + r

            @pl.when(i < bins)
            def _():
                put_own(i)

        return matmul(b, *carry)

    zero = jnp.zeros((8, chans), F32)
    acc_s, acc_q = lax.fori_loop(0, blocks, step, (zero, zero))
    moments[0:1, 0:chans] = jnp.sum(acc_s, axis=0, keepdims=True)
    moments[0:1, chans : 2 * chans] = jnp.sum(acc_q, axis=0, keepdims=True)


def mel_kernel(bins, frames, count, info, const, stats, gain, shift, first_out, weights, base, noisy, mel, mel_in, sums):
    chans = first_out.shape[-1]
    width = frames + 2 * EDGE
    tm, tms, fq, fqs = info[0], info[1], info[2], info[3]
    mean, scale = norm_terms(stats[...], gain[...], count)
    shift_v = shift[...]
    place = lax.broadcasted_iota(jnp.int32, (width, 1), 0) - EDGE + tm * frames
    inside = jnp.where((place >= 0) & (place < frames * tms), 1.0, 0.0).astype(F32)
    inside = jnp.broadcast_to(inside, (width, chans))
    sums[...] = jnp.zeros_like(sums)

    def row(r, _):
        bin_ok = ((r > 0) | (fq > 0)) & ((r < bins + 1) | (fq < fqs - 1))
        ok = jnp.where(bin_ok, 1.0, 0.0).astype(F32)
        val = half_silu(first_out[r].astype(F32), mean, scale, shift_v)
        val = jnp.where(inside * ok > 0.0, val, 0.0).astype(BF16)
        taps = nt(weights[...], val)
        taps = taps[0:24] + taps[24:48] + taps[48:72]
        w = width
        sums[pl.ds(pl.multiple_of((r + 2) * 8, 8), 8), 0:w] = taps[0:8]
        at = pl.multiple_of((r + 1) * 8, 8)
        sums[pl.ds(at, 8), 0:w] = sums[pl.ds(at, 8), 0:w] + taps[8:16]
        at = pl.multiple_of(r * 8, 8)
        sums[pl.ds(at, 8), 0:w] = sums[pl.ds(at, 8), 0:w] + taps[16:24]
        return 0

    lax.fori_loop(0, bins + 2, row, 0, unroll=6)
    lanes = sums.shape[1]
    t0 = sums[pl.ds(16, bins, stride=8), :]
    t1 = sums[pl.ds(17, bins, stride=8), :]
    t2 = sums[pl.ds(18, bins, stride=8), :]
    b1 = base[pl.ds(1, bins, stride=8), :]
    vel = pltpu.roll(t0, 1, 1) + t1 + pltpu.roll(t2, lanes - 1, 1)
    vel = vel + (b1 + const[0])
    res = noisy[...] + STEP_SIZE * vel
    at = lax.broadcasted_iota(jnp.int32, (bins, lanes), 1) - EDGE
    pos = at + tm * frames
    good = (at >= -4) & (at < frames + 4) & (pos >= 0) & (pos < frames * tms)
    mel[...] = res
    mel_in[...] = jnp.where(good, res, 0.0).astype(BF16)


def up_kernel(frames, info, mel, pre_w, pre_b, up_w, up_b, perm, vocal, cols, wide, acc):
    step = pl.program_id(0)
    tm, tms = info[0], info[1]
    taps = pre_w.shape[1]

    @pl.when(step == 0)
    def _():
        melt = mel[...].astype(F32).T
        rows = [melt[4 + q : 4 + q + frames].astype(BF16) for q in range(taps + 2)]
        for s in range(3):
            cols[s * frames : (s + 1) * frames, :] = jnp.concatenate(rows[s : s + taps], axis=1)
        acc[...] = jnp.zeros_like(acc)

    slabs, _, depth, bins = pre_w.shape
    rhs = jnp.concatenate(
        [jnp.concatenate([pre_w[s, k] for k in range(taps)], axis=1) for s in range(slabs)], axis=0
    )
    feats = nt(cols[...], rhs) + pre_b[0]
    line = lax.broadcasted_iota(jnp.int32, (3 * frames, 1), 0)
    pos = tm * frames + line % frames + line // frames - 1
    good = (pos >= 0) & (pos < frames * tms)
    feats = jnp.where(good, feats, 0.0).astype(BF16)
    count, phases, outs = up_w.shape
    for c in range(outs // 128):
        wide[c] = up_w[:, :, c * 128 : (c + 1) * 128].astype(F32).reshape(count * phases, 128)
    for k in range(phases):
        w = [wide.at[c][pl.ds(k, count, stride=phases), :] for c in range(outs // 128)]
        w = jnp.concatenate(w, axis=1).astype(BF16)
        p = (k + 2) % 4
        s = 2 if k < 2 else (1 if k < 6 else 0)
        part = jnp.dot(feats[s * frames : (s + 1) * frames], w, preferred_element_type=F32)
        acc[p * frames : (p + 1) * frames, :] += part

    @pl.when(step == pl.num_programs(0) - 1)
    def _():
        done = (acc[...] + up_b[...]).astype(BF16)
        res = lax.dot_general(done, perm[...], (((0,), (0,)), ((), ())), preferred_element_type=F32)
        vocal[...] = res.astype(BF16)


def exchange(sums):
    devices = lax.axis_size("tm") * lax.axis_size("freq")
    sent = jnp.broadcast_to(sums, (devices, sums.shape[-1]))
    return lax.all_to_all(sent, ("tm", "freq"), 0, 0, tiled=True)


def neighbours(axis):
    n = lax.axis_size(axis)
    up = [(i, i + 1) for i in range(n - 1)]
    return up, [(j, i) for i, j in up]


def shards(
    latent,
    mel_noisy,
    time_shift,
    first_gain,
    first_shift,
    conv_first,
    second_gain,
    second_shift,
    conv_second,
    second_bias,
    out_proj,
    pre_weight,
    pre_bias,
    up_weight,
    up_bias,
):
    chans, bins, frames = latent.shape
    tms, fqs = lax.axis_size("tm"), lax.axis_size("freq")
    tm, fq = lax.axis_index("tm"), lax.axis_index("freq")
    count = float(chans // GROUPS * bins * frames * tms * fqs)
    width = frames + 2 * EDGE
    lanes = -(-width // 128) * 128
    info = jnp.stack([tm, jnp.int32(tms), fq, jnp.int32(fqs)])
    up, down = neighbours("tm")
    x = jnp.transpose(latent, (1, 2, 0))

    if fqs == 2:
        swap = lax.ppermute(jnp.where(fq == 0, x[bins - 2 :], x[:2]), "freq", [(0, 1), (1, 0)])
        top = bottom = swap
    else:
        fup, fdown = neighbours("freq")
        top = lax.ppermute(x[bins - 2 :], "freq", fup)
        bottom = lax.ppermute(x[:2], "freq", fdown)
    last = jnp.concatenate([top[:, frames - EDGE :], x[:, frames - EDGE :], bottom[:, frames - EDGE :]], axis=0)
    first = jnp.concatenate([top[:, :EDGE], x[:, :EDGE], bottom[:, :EDGE]], axis=0)
    left = lax.ppermute(last, "tm", up)
    right = lax.ppermute(first, "tm", down)
    noisy_left = lax.ppermute(mel_noisy[:, frames - EDGE :], "tm", up)
    noisy_right = lax.ppermute(mel_noisy[:, :EDGE], "tm", down)
    noisy = jnp.concatenate(
        [noisy_left, mel_noisy, noisy_right, jnp.zeros((bins, lanes - width), F32)], axis=1
    )

    x32 = x.astype(F32)
    sums = jnp.concatenate([jnp.sum(x32, axis=(0, 1)), jnp.sum(x32 * x32, axis=(0, 1))])[None]
    stats = exchange(sums)

    proj = jnp.stack(split3(out_proj))[:, None, :]
    proj8 = jnp.concatenate([jnp.zeros_like(proj), proj, jnp.zeros((3, 6, chans), BF16)], axis=1).reshape(24, chans)
    rows = 6
    while (bins + 2) % rows:
        rows -= 1
    first_out, moments, base = pl.pallas_call(
        functools.partial(conv_kernel, bins, frames, rows, count),
        out_shape=(
            jax.ShapeDtypeStruct((bins + 2, width, chans), BF16),
            jax.ShapeDtypeStruct((1, 2 * chans), F32),
            jax.ShapeDtypeStruct((bins, 8, width), F32),
        ),
        in_specs=[SMEM] + [VMEM] * 11,
        out_specs=(VMEM,) * 3,
        scratch_shapes=[pltpu.VMEM((bins + 4, width, 3 * chans), BF16)],
        name="conv_first",
    )(
        info, stats, first_gain[None], first_shift[None], time_shift[None], x, left, right, top, bottom,
        conv_first.reshape(9 * chans, chans), proj8,
    )
    stats2 = exchange(moments)

    folded = jnp.einsum("ijco,o->ijc", conv_second.astype(F32), out_proj, precision=lax.Precision.HIGHEST)
    folded = jnp.concatenate([folded, jnp.zeros((3, 5, chans), F32)], axis=1).reshape(24, chans)
    folded = jnp.concatenate(split3(folded), axis=0)
    const = jnp.sum(second_bias * out_proj)[None]
    base = jnp.pad(base.reshape(bins * 8, width), ((0, 0), (0, lanes - width)))
    mel, mel_in = pl.pallas_call(
        functools.partial(mel_kernel, bins, frames, count),
        out_shape=(jax.ShapeDtypeStruct((bins, lanes), F32), jax.ShapeDtypeStruct((bins, lanes), BF16)),
        in_specs=[SMEM, SMEM] + [VMEM] * 7,
        out_specs=(VMEM,) * 2,
        scratch_shapes=[pltpu.VMEM(((bins + 4) * 8, lanes), F32)],
        name="mel",
    )(info, const, stats2, second_gain[None], second_shift[None], first_out, folded, base, noisy)
    mel_next = mel[:, EDGE : EDGE + frames]
    mel_full = lax.all_gather(mel_in, "freq", axis=0, tiled=True)

    taps = pre_weight.shape[1]
    depth = pre_weight.shape[0]
    pieces = lax.all_gather(jnp.transpose(pre_weight, (1, 0, 2)), "tm", axis=0, tiled=False)
    slabs = 1
    while slabs * depth < 384 or tms % slabs:
        slabs += 1
    outs = up_weight.shape[2]
    source = jnp.arange(4 * frames)
    perm = (source[:, None] % frames * 4 + source[:, None] // frames == source[None, :]).astype(BF16)
    vocal = pl.pallas_call(
        functools.partial(up_kernel, frames),
        out_shape=jax.ShapeDtypeStruct((outs, 4 * frames), BF16),
        grid_spec=pltpu.PrefetchScalarGridSpec(
            num_scalar_prefetch=1,
            grid=(tms // slabs,),
            in_specs=[
                pl.BlockSpec((fqs * bins, lanes), lambda i, s: (0, 0)),
                pl.BlockSpec((slabs, taps, depth, fqs * bins), lambda i, s: (i, 0, 0, 0)),
                pl.BlockSpec((1, 1, slabs * depth), lambda i, s: (i, 0, 0)),
                pl.BlockSpec((slabs * depth, up_weight.shape[1], outs), lambda i, s: (i, 0, 0)),
                pl.BlockSpec((1, outs), lambda i, s: (0, 0)),
                pl.BlockSpec((4 * frames, 4 * frames), lambda i, s: (0, 0)),
            ],
            out_specs=pl.BlockSpec((outs, 4 * frames), lambda i, s: (0, 0)),
            scratch_shapes=[
                pltpu.VMEM((3 * frames, taps * fqs * bins), BF16),
                pltpu.VMEM((outs // 128, slabs * depth * up_weight.shape[1], 128), F32),
                pltpu.VMEM((4 * frames, outs), F32),
            ],
        ),
        name="up",
    )(info, mel_full, pieces, pre_bias.reshape(tms // slabs, 1, slabs * depth), up_weight, up_bias[None], perm)
    return (mel_next, vocal)


def solution(mesh):
    in_specs = (
        P(None, "freq", ("song", "tm")),
        P("freq", ("song", "tm")),
        P("song"),
        P(),
        P(),
        P(),
        P(),
        P(),
        P(),
        P(),
        P(),
        P("tm", None, None),
        P(),
        P(None, None, "freq"),
        P("freq"),
    )
    out_specs = (P("freq", ("song", "tm")), P("freq", ("song", "tm")))
    return jax.shard_map(shards, mesh=mesh, in_specs=in_specs, out_specs=out_specs, check_vma=False)
```

time: 245 us -> 116 us (0.47)
  matrix products: 76.5 us -> 1.04 us
  blocking collectives: 70.9 us -> 3.13 us
  local copies, waits for them, and re-layouts: 49.7 us -> 9.65 us
  Pallas kernels: 0 us -> 38.6 us
  starting transfers between devices: 13.8 us -> 25.6 us
  waiting for transfers between devices: 4.92 us -> 16.2 us
  other arithmetic: 14.3 us -> 7.14 us
    dot_general x33 -> x1, matrix products: 76.5 us -> 1.04 us  [shards(): jnp.einsum('ijco,o->ijc', conv_second.astype(F32), out_proj, precision=la...]
    psum x2 -> x0, blocking collectives: 68.3 us -> none  [group_moments(): first, second = lax.psum((first, second), ('tm', 'freq'))]
    slice x4, local copies, waits for them, and re-layouts: 44.5 us -> 2.6 us  [the longest x1 1.45 us: shards(): mel_next = mel[:, EDGE:EDGE + frames]]
    pallas_call x0 -> x3, Pallas kernels: none -> 38.6 us  [the longest x1 21.5 us: shards(): pl.pallas_call(functools.partial(conv_kernel, bins, frames, rows, count),...]
    all_to_all x0 -> x2, starting transfers between devices: none -> 13.5 us  [exchange(): return lax.all_to_all(sent, ('tm', 'freq'), 0, 0, tiled=True)]
    ppermute x10 -> x5, waiting for transfers between devices: 4.9 us -> 11.3 us  [the longest x1 11.2 us: shards(): left = lax.ppermute(last, 'tm', up)]
    convert_element_type x4 -> x3, other arithmetic: 5.9 us -> 1.36 us  [the longest x1 0.75 us: shards(): (source[:, None] % frames * 4 + source[:, None] // frames == source[None,...]
    concatenate x2 -> x5, other arithmetic: 5.65 us -> 1.41 us  [the longest x1 0.71 us: shards(): jnp.concatenate([noisy_left, mel_noisy, noisy_right, jnp.zeros((bins, lan...]
  transfers between devices with their start and end apart: 11 -> 8, of which waited for: 3 -> 2; matrix products, arithmetic and copies ran while one was open for 49% -> 15% of each run, Pallas kernels for 0% -> 24%
where the time goes in v1:
time: 116 us
  Pallas kernels  38.6 us (33%)
  starting transfers between devices  25.6 us (22%)
  waiting for transfers between devices  16.2 us (14%)
  between operations  14.3 us (12%)
  local copies, waits for them, and re-layouts  9.65 us (8%)
  other arithmetic  7.14 us (6%)
  blocking collectives  3.13 us (3%)
    pallas_call x1, Pallas kernels, shards(): pl.pallas_call(functools.partial(conv_kernel, bins, frames, rows, count),...  21.5 us
    all_to_all x2, starting transfers between devices, exchange(): return lax.all_to_all(sent, ('tm', 'freq'), 0, 0, tiled=True)  13.5 us
    ppermute x1, waiting for transfers between devices, shards(): left = lax.ppermute(last, 'tm', up)  11.2 us
    pallas_call x1, Pallas kernels, shards(): pl.pallas_call(functools.partial(up_kernel, frames), out_shape=jax.ShapeD...  10.3 us
    pallas_call x1, Pallas kernels, shards(): pl.pallas_call(functools.partial(mel_kernel, bins, frames, count), out_sh...  6.79 us
    ppermute x1, starting transfers between devices, shards(): noisy_left = lax.ppermute(mel_noisy[:, frames - EDGE:], 'tm', up)  4.55 us
    ppermute x1, starting transfers between devices, shards(): left = lax.ppermute(last, 'tm', up)  4.45 us
    all_to_all x2, waiting for transfers between devices, exchange(): return lax.all_to_all(sent, ('tm', 'freq'), 0, 0, tiled=True)  4.22 us
  transfers between devices with their start and end apart: 8, of which 2 were waited for; matrix products, arithmetic and copies ran while one was open for 15% of the time, Pallas kernels for 24%

profile of v1, /device:TPU:0, one launch (start us, length us, event | category | flops | bytes accessed | tf_op | source)
XLA Modules:
  0.0 115.5 jit_solution(7292678492817271115)
XLA Ops:
  7.2 0.0 copy-start
  7.2 0.0 copy-start.2
  7.2 0.0 copy-start.6
  7.2 0.0 copy-start.8
  7.2 0.0 all-gather.3.cloned.1.call-start
  7.3 0.7 all-gather.3.cloned.1.call-update
  7.9 2.2 %convert_reduce_fusion = (f32[256]{0:T(256)S(1)}, f32[256]{0:T(256)S(1)}) fusion(bf16[256,64,64]{0,2,1:T(8,128)(2,1)} %param.15), kind=kLoop, calls=%fused_computation.1 | loop fusion | flops 4193792 | bytes 2099200 | tf_op jit(solution)/shard_map/reduce_sum | solution.py:264
  10.1 0.0 copy-start.5
  10.1 0.0 copy-start.7
  10.2 0.6 broadcast_in_dim.49
  10.8 7.4 %all-to-all-start = ((f32[16,1,512]{2,1,0:T(1,128)}), f32[16,1,512]{2,1,0:T(1,128)S(1)}, u32[]{:S(2)}, u32[]{:S(2)}) async-start(f32[16,1,512]{2,1,0:T(1,128)} %broadcast_in_dim.49), calls=%async_computation | async-start | bytes 65536 | tf_op jit(solution)/shard_map/all_to_all | solution.py:210
  18.2 0.9 slice_select_fusion
  19.1 0.5 collective-permute-start
  19.6 0.0 copy-done.2
  19.6 0.1 fusion.10
  19.6 1.3 %collective-permute-start.4 = (f32[64,8]{1,0:T(8,128)S(1)}, f32[64,8]{1,0:T(8,128)S(1)}, u32[]{:S(2)}, u32[]{:S(2)}) collective-permute-start(f32[64,8]{1,0:T(8,128)S(1)} %get-tuple-element.19), channel_id=1, source_target_pairs={{2,0},{4,2},{6,4},{8,6},{10,8},{12,10},{14,12},{3,1},{5,3},{7,5},{... | collective-permute-start | bytes 6152 | tf_op jit(solution)/shard_map/ppermute | solution.py:258
  20.9 4.5 %collective-permute-start.3 = (f32[64,8]{1,0:T(8,128)S(1)}, f32[64,8]{1,0:T(8,128)S(1)}, u32[]{:S(2)}, u32[]{:S(2)}) collective-permute-start(f32[64,8]{1,0:T(8,128)S(1)} %get-tuple-element.18), channel_id=1, source_target_pairs={{0,2},{2,4},{4,6},{6,8},{8,10},{10,12},{12,14},{1,3},{3,5},{5,7},{... | collective-permute-start | bytes 6152 | tf_op jit(solution)/shard_map/ppermute | solution.py:257
  25.5 0.0 copy-done.6
  25.5 0.0 copy-done.8
  25.5 0.6 fusion.11
  26.2 0.1 pad.15.clone
  26.2 0.0 copy-done
  26.3 1.0 fusion.12
  27.3 0.7 maximum_bitcast_fusion.proj
  28.0 0.8 fusion.1.perm
  28.8 1.1 fusion.8
  29.8 0.0 collective-permute-done.top.bottom
  29.9 0.0 copy-start.1
  29.9 4.5 %collective-permute-start.1 = (bf16[68,8,256]{2,1,0:T(8,128)(2,1)S(1)}, bf16[68,8,256]{2,1,0:T(8,128)(2,1)S(1)}, u32[]{:S(2)}, u32[]{:S(2)}) collective-permute-start(bf16[68,8,256]{2,1,0:T(8,128)(2,1)S(1)} %pad_maximum_fusion), channel_id=1, source_target_pairs={{0,2},{2,4},{4,6},{6,8},{8,10},{10,12},{12,14},{1,3},{3,5},{5,7},{... | collective-permute-start | bytes 835592 | tf_op jit(solution)/shard_map/ppermute | solution.py:255
  34.4 1.3 %collective-permute-start.2 = (bf16[68,8,256]{2,1,0:T(8,128)(2,1)S(1)}, bf16[68,8,256]{2,1,0:T(8,128)(2,1)S(1)}, u32[]{:S(2)}, u32[]{:S(2)}) collective-permute-start(bf16[68,8,256]{2,1,0:T(8,128)(2,1)S(1)} %pad_maximum_fusion.1), channel_id=1, source_target_pairs={{2,0},{4,2},{6,4},{8,6},{10,8},{12,10},{14,12},{3,1},{5,3},{7,5},{... | collective-permute-start | bytes 835592 | tf_op jit(solution)/shard_map/ppermute | solution.py:256
  35.7 0.6 pad_maximum_fusion.2.weights
  36.4 0.6 pad_add_fusion.info
  37.0 0.0 copy-done.5
  37.0 0.6 reshape.90.pre_b
  37.6 0.0 copy-done.7
  37.6 0.6 broadcast_in_dim.60.up_b
  38.2 0.1 pad.9.clone
  38.2 0.0 all-to-all-done
  38.2 0.6 copy.27
  38.9 11.2 %collective-permute-done.1.left = bf16[68,8,256]{2,1,0:T(8,128)(2,1)S(1)} collective-permute-done((bf16[68,8,256]{2,1,0:T(8,128)(2,1)S(1)}, bf16[68,8,256]{2,1,0:T(8,128)(2,1)S(1)}, u32[]{:S(2)}, u32[]{:S(2)}) %collective-permute-start.1) | collective-permute-done | bytes 278560 | tf_op jit(solution)/shard_map/ppermute | solution.py:255
  50.1 0.0 copy-start.3
  50.1 0.0 collective-permute-done.2.right
  50.1 0.0 copy-start.4
  50.1 0.0 copy-done.1
  50.1 0.7 copy-done.3
  50.8 0.1 copy-done.4
  50.9 21.5 %conv_first.1 = (bf16[66,80,256]{2,1,0:T(8,128)(2,1)}, f32[1,512]{1,0:T(1,128)}, f32[64,8,80]{2,1,0:T(8,128)}) custom-call(s32[4]{0:T(128)} %pad_add_fusion.info, f32[16,512]{1,0:T(8,128)} %bitcast.55, f32[1,256]{1,0:T(1,128)} %bitcast.63, f32[1,256]{1,0:T(1,128)} %bitcast.64, f32[1,256]{1,0:T(1,128)} %bitcast.65, bf16[64,64,256]{2,1,0:T(8,128)(2,1)} %bitcast.50, ...), custom_call_target="tpu_custom_call" | custom-call | tf_op jit(solution)/shard_map/conv_first/pallas_call | solution.py:272
  72.4 1.3 %broadcast_in_dim.56 = f32[16,1,512]{2,1,0:T(1,128)} broadcast(f32[512]{0:T(512)} %bitcast.60), dimensions={2} | broadcast | bytes 34816 | tf_op jit(solution)/shard_map/broadcast_in_dim | solution.py:209
  73.7 6.1 %all-to-all-start.1 = ((f32[16,1,512]{2,1,0:T(1,128)}), f32[16,1,512]{2,1,0:T(1,128)S(1)}, u32[]{:S(2)}, u32[]{:S(2)}) async-start(f32[16,1,512]{2,1,0:T(1,128)} %broadcast_in_dim.56), calls=%async_computation.1 | async-start | bytes 65536 | tf_op jit(solution)/shard_map/all_to_all | solution.py:210
  79.8 0.0 collective-permute-done.4
  79.8 0.0 collective-permute-done.3
  79.8 0.7 maximum_maximum_fusion.noisy
  80.5 1.7 %pad.5.base = f32[512,128]{1,0:T(8,128)} pad(f32[512,80]{1,0:T(8,128)} %bitcast.54, f32[]{:T(128)} %constant.45.clone.1), padding=0_0x0_48 | pad | bytes 425988 | tf_op jit(solution)/shard_map/jit(_pad)/pad | solution.py:293
  82.2 4.2 %all-to-all-done.1 = f32[16,1,512]{2,1,0:T(1,128)S(1)} async-done(((f32[16,1,512]{2,1,0:T(1,128)}), f32[16,1,512]{2,1,0:T(1,128)S(1)}, u32[]{:S(2)}, u32[]{:S(2)}) %all-to-all-start.1) | async-done | bytes 32800 | tf_op jit(solution)/shard_map/all_to_all | solution.py:210
  86.4 0.6 copy.26
  87.0 6.8 %mel.1 = (f32[64,128]{1,0:T(8,128)}, bf16[64,128]{1,0:T(8,128)(2,1)}) custom-call(s32[4]{0:T(128)} %pad_add_fusion.info, f32[1]{0:T(128)} %bitcast.2.const, f32[16,512]{1,0:T(8,128)} %bitcast.56, f32[1,256]{1,0:T(1,128)} %bitcast.61, f32[1,256]{1,0:T(1,128)} %bitcast.62, bf16[66,80,256]{2,1,0:T(8,128)(2,1)} %get-tuple-element.8.first_out, ...), custom_call_target="tpu_custom_call" | custom-call | tf_op jit(solution)/shard_map/mel/pallas_call | solution.py:294
  93.8 1.4 %slice.37 = f32[64,64]{1,0:T(8,128)} slice(f32[64,128]{1,0:T(8,128)} %get-tuple-element.10), slice={[0:64], [8:72]} | slice | bytes 32768 | tf_op jit(solution)/shard_map/slice | solution.py:302
  95.3 3.1 %all_gather.9.mel = bf16[128,128]{1,0:T(8,128)(2,1)} all-gather(bf16[64,128]{1,0:T(8,128)(2,1)} %get-tuple-element.11), channel_id=1, replica_groups=mesh['song'=2,'tm'=8,'freq'=2] {'freq'}, dimensions={0}, use_global_device_ids=true | all-gather | bytes 49152 | tf_op jit(solution)/shard_map/all_gather | solution.py:303
  98.4 0.0 all-gather.3.cloned.1.call-done
  98.4 10.3 %up.1 = bf16[384,256]{1,0:T(8,128)(2,1)} custom-call(s32[4]{0:T(128)} %pad_add_fusion.info, bf16[128,128]{1,0:T(8,128)(2,1)} %all_gather.9.mel, bf16[8,7,192,128]{3,2,1,0:T(8,128)(2,1)} %bitcast.51, f32[4,1,384]{2,1,0:T(1,128)} %reshape.90.pre_b, bf16[1536,8,384]{2,1,0:T(8,128)(2,1)} %up_w.1, f32[1,384]{1,0:T(1,128)} %broadcast_in_dim.60.up_b, ...), custom_call_target="tpu_custom_call" | custom-call | tf_op jit(solution)/shard_map/up/pallas_call | solution.py:314
  (16 shorter events, 0.2 us)
Async XLA Ops:
  7.2 19.1 %copy-start = (bf16[3,3,256,256]{3,2,1,0:T(8,128)(2,1)S(1)}, bf16[3,3,256,256]{3,2,1,0:T(8,128)(2,1)}, u32[]{:S(2)}) copy-start(bf16[3,3,256,256]{3,2,1,0:T(8,128)(2,1)} %param.23) | copy-start | bytes 3538948
  7.2 12.4 %copy-start.2 = (f32[64,64]{1,0:T(8,128)S(1)}, f32[64,64]{1,0:T(8,128)}, u32[]{:S(2)}) copy-start(f32[64,64]{1,0:T(8,128)} %param.16) | copy-start | bytes 49156
  7.2 18.3 %copy-start.6 = (f32[256]{0:T(256)S(1)}, f32[256]{0:T(256)}, u32[]{:S(2)}) copy-start(f32[256]{0:T(256)} %param.25) | copy-start | bytes 3076
  7.2 18.3 %copy-start.8 = (f32[256]{0:T(256)S(1)}, f32[256]{0:T(256)}, u32[]{:S(2)}) copy-start(f32[256]{0:T(256)} %param.24) | copy-start | bytes 3076
  7.2 91.2 %all-gather.3.cloned.1.call-start = ((), (), s32[]{:S(2)}) async-start(), calls=%async_computation.2 | async-start | bytes 3096576 | tf_op jit(solution)/shard_map/all_gather | solution.py:307
  10.1 26.8 %copy-start.5 = (f32[1536]{0:T(1024)S(1)}, f32[1536]{0:T(1024)}, u32[]{:S(2)}) copy-start(f32[1536]{0:T(1024)} %param.27) | copy-start | bytes 18436
  10.1 27.4 %copy-start.7 = (f32[384]{0:T(512)S(1)}, f32[384]{0:T(512)}, u32[]{:S(2)}) copy-start(f32[384]{0:T(512)} %param.29) | copy-start | bytes 4612
  10.8 27.4 %all-to-all-start = ((f32[16,1,512]{2,1,0:T(1,128)}), f32[16,1,512]{2,1,0:T(1,128)S(1)}, u32[]{:S(2)}, u32[]{:S(2)}) async-start(f32[16,1,512]{2,1,0:T(1,128)} %broadcast_in_dim.49), calls=%async_computation | async-start | bytes 65536 | tf_op jit(solution)/shard_map/all_to_all | solution.py:210
  19.1 10.7 %collective-permute-start = (bf16[2,64,256]{2,1,0:T(8,128)(2,1)S(1)}, bf16[2,64,256]{2,1,0:T(8,128)(2,1)S(1)}, u32[]{:S(2)}, u32[]{:S(2)}) collective-permute-start(bf16[2,64,256]{2,1,0:T(8,128)(2,1)S(1)} %slice_select_fusion), channel_id=1, source_target_pairs={{0,1},{1,0},{2,3},{3,2},{4,5},{5,4},{6,7},{7,6},{8,9},{9,8},{10,11... | collective-permute-start | bytes 196616 | tf_op jit(solution)/shard_map/ppermute | solution.py:247
  19.6 60.1 %collective-permute-start.4 = (f32[64,8]{1,0:T(8,128)S(1)}, f32[64,8]{1,0:T(8,128)S(1)}, u32[]{:S(2)}, u32[]{:S(2)}) collective-permute-start(f32[64,8]{1,0:T(8,128)S(1)} %get-tuple-element.19), channel_id=1, source_target_pairs={{2,0},{4,2},{6,4},{8,6},{10,8},{12,10},{14,12},{3,1},{5,3},{7,5},{... | collective-permute-start | bytes 6152 | tf_op jit(solution)/shard_map/ppermute | solution.py:258
  20.9 58.8 %collective-permute-start.3 = (f32[64,8]{1,0:T(8,128)S(1)}, f32[64,8]{1,0:T(8,128)S(1)}, u32[]{:S(2)}, u32[]{:S(2)}) collective-permute-start(f32[64,8]{1,0:T(8,128)S(1)} %get-tuple-element.18), channel_id=1, source_target_pairs={{0,2},{2,4},{4,6},{6,8},{8,10},{10,12},{12,14},{1,3},{3,5},{5,7},{... | collective-permute-start | bytes 6152 | tf_op jit(solution)/shard_map/ppermute | solution.py:257
  29.9 20.3 %copy-start.1 = (bf16[2,64,256]{2,1,0:T(8,128)(2,1)}, bf16[2,64,256]{2,1,0:T(8,128)(2,1)S(1)}, u32[]{:S(2)}) copy-start(bf16[2,64,256]{2,1,0:T(8,128)(2,1)S(1)} %collective-permute-done.top.bottom) | copy-start | bytes 196612
  29.9 20.2 %collective-permute-start.1 = (bf16[68,8,256]{2,1,0:T(8,128)(2,1)S(1)}, bf16[68,8,256]{2,1,0:T(8,128)(2,1)S(1)}, u32[]{:S(2)}, u32[]{:S(2)}) collective-permute-start(bf16[68,8,256]{2,1,0:T(8,128)(2,1)S(1)} %pad_maximum_fusion), channel_id=1, source_target_pairs={{0,2},{2,4},{4,6},{6,8},{8,10},{10,12},{12,14},{1,3},{3,5},{5,7},{... | collective-permute-start | bytes 835592 | tf_op jit(solution)/shard_map/ppermute | solution.py:255
  34.4 15.7 %collective-permute-start.2 = (bf16[68,8,256]{2,1,0:T(8,128)(2,1)S(1)}, bf16[68,8,256]{2,1,0:T(8,128)(2,1)S(1)}, u32[]{:S(2)}, u32[]{:S(2)}) collective-permute-start(bf16[68,8,256]{2,1,0:T(8,128)(2,1)S(1)} %pad_maximum_fusion.1), channel_id=1, source_target_pairs={{2,0},{4,2},{6,4},{8,6},{10,8},{12,10},{14,12},{3,1},{5,3},{7,5},{... | collective-permute-start | bytes 835592 | tf_op jit(solution)/shard_map/ppermute | solution.py:256
  50.1 0.7 copy-start.3
  50.1 0.8 copy-start.4
  73.7 12.7 %all-to-all-start.1 = ((f32[16,1,512]{2,1,0:T(1,128)}), f32[16,1,512]{2,1,0:T(1,128)S(1)}, u32[]{:S(2)}, u32[]{:S(2)}) async-start(f32[16,1,512]{2,1,0:T(1,128)} %broadcast_in_dim.56), calls=%async_computation.1 | async-start | bytes 65536 | tf_op jit(solution)/shard_map/all_to_all | solution.py:210
Sparse Core Ops, SparseCore 0:
  10.2 63.4 all-gather.2

commit v2 on v0

v2 whole, which is shorter than its diff:
```python
import functools

import jax
import jax.numpy as jnp
from jax import lax
from jax.experimental import pallas as pl
from jax.experimental.pallas import tpu as pltpu
from jax.sharding import PartitionSpec as P


GROUPS = 32
EPSILON = 1e-05
STEP_SIZE = 0.25
EDGE = 8
F32 = jnp.float32
BF16 = jnp.bfloat16
VMEM = pl.BlockSpec(memory_space=pltpu.VMEM)
SMEM = pl.BlockSpec(memory_space=pltpu.SMEM)


def nt(a, b):
    return lax.dot_general(a, b, (((1,), (1,)), ((), ())), preferred_element_type=F32)


def split3(x):
    hi = x.astype(BF16)
    rest = x - hi.astype(F32)
    mid = rest.astype(BF16)
    low = (rest - mid.astype(F32)).astype(BF16)
    return hi, mid, low


def norm_terms(stats, gain, shift, count):
    chans = stats.shape[2]
    total = jnp.sum(stats, axis=0)
    if total.shape[0] < 8:
        total = jnp.concatenate([total, jnp.zeros((8 - total.shape[0], chans), F32)], axis=0)
    size = chans // GROUPS
    rows = lax.broadcasted_iota(jnp.int32, (chans, chans), 0) // size
    cols = lax.broadcasted_iota(jnp.int32, (chans, chans), 1) // size
    same = jnp.where(rows == cols, 1.0, 0.0).astype(F32)
    keep = lax.broadcasted_iota(jnp.int32, (8, chans), 0) < 2
    both = jnp.where(keep, total, 0.0)
    groups = lax.dot_general(
        both, same, (((1,), (0,)), ((), ())), precision=lax.Precision.HIGHEST, preferred_element_type=F32
    )
    mean = groups[0:1] / count
    var = groups[1:2] / count - mean * mean
    half = 0.5 * lax.rsqrt(var + EPSILON) * gain
    return half, 0.5 * shift - mean * half


def act_fn(values, scale, shift):
    half = values * scale + shift
    return half + half * jnp.tanh(half)


def edge_flags(axis):
    index = lax.axis_index(axis)
    return (
        jnp.where(index > 0, 1.0, 0.0).astype(F32),
        jnp.where(index < lax.axis_size(axis) - 1, 1.0, 0.0).astype(F32),
    )


def place_rows(rows, begin, chans):
    count, lanes = rows.shape
    rows = jnp.concatenate([rows, jnp.zeros((count, chans - lanes), F32)], axis=1) if lanes < chans else rows
    return jnp.concatenate(
        [jnp.zeros((n, chans), F32) if i != 1 else rows for i, n in enumerate((begin, 0, 8 - begin - count)) if i == 1 or n],
        axis=0,
    )


def sums_kernel(values, noisy, out, last, first):
    rows, frames, chans = values.shape

    def step(r, carry):
        line = values[r]
        last[r] = line[frames - EDGE :]
        first[r] = line[:EDGE]
        x = line.astype(F32).reshape(frames // 8, 8, chans)
        return carry[0] + jnp.sum(x, axis=0), carry[1] + jnp.sum(x * x, axis=0)

    zero = jnp.zeros((8, chans), F32)
    one, two = lax.fori_loop(0, rows, step, (zero, zero), unroll=8)
    both = place_rows(
        jnp.concatenate([jnp.sum(one, axis=0, keepdims=True), jnp.sum(two, axis=0, keepdims=True)], axis=0), 0, chans
    )
    old = noisy[...].T
    to_right = place_rows(old[frames - 4 :], 2, chans)
    to_left = place_rows(old[:4], 2, chans)
    fqs = lax.axis_size("freq")
    me = lax.axis_index("tm") * fqs + lax.axis_index("freq")
    for d in range(out.shape[0]):
        right = jnp.where(me + fqs == d, 1.0, 0.0).astype(F32)
        left = jnp.where(me - fqs == d, 1.0, 0.0).astype(F32)
        out[d] = both + to_right * right + to_left * left


def conv_kernel(bins, frames, rows, count, stats, small, own, left, right, edges,
                weight, out, moments, base, act, made, sems):
    chans = own.shape[-1]
    width = frames + 2 * EDGE
    scale, shift = norm_terms(stats[...], small[0:1], small[1:2], count)
    tshift = small[2:3]
    proj = jnp.concatenate([jnp.broadcast_to(p, (8, chans)) for p in split3(small[5:6])], axis=0)
    has_left, has_right = edge_flags("tm")
    has_top, has_bottom = edge_flags("freq")

    def put(dest, lhs, middle, rhs, bin_ok):
        l32, m32, r32 = lhs.astype(F32), middle.astype(F32), rhs.astype(F32)
        val = jnp.concatenate(
            [
                act_fn(l32, scale, shift) * has_left,
                act_fn(m32, scale, shift),
                act_fn(r32, scale, shift) * has_right,
            ],
            axis=0,
        )
        if bin_ok is not None:
            val = val * bin_ok
        dest[:, 0:chans] = pltpu.roll(val, 1, 0).astype(BF16)
        dest[:, chans : 2 * chans] = val.astype(BF16)
        dest[:, 2 * chans : 3 * chans] = pltpu.roll(val, width - 1, 0).astype(BF16)
        return jnp.concatenate([l32, m32, r32], axis=0).astype(BF16)

    def put_own(dest, i):
        raw = put(dest, left[i], own[i], right[i], None)
        parts = nt(proj, raw)
        base[pl.ds(i, 1), 0:width] = parts[0:1] + parts[8:9] + parts[16:17]

    def put_edge(row, i, flag):
        line = edges[i]
        put(act.at[row], line[:EDGE], line[EDGE : EDGE + frames], line[EDGE + frames :], flag)

    put_edge(0, 0, has_top)
    put_edge(1, 1, has_top)
    for i in range(rows):
        put_own(act.at[i + 2], i)

    blocks = (bins + 2) // rows

    def send(first):
        part = pl.ds(first, rows)
        return pltpu.make_async_copy(made.at[part], out.at[part], sems.at[first // rows])

    def matmul(window, first, acc_s, acc_q):
        lhs = jnp.concatenate([window[i : i + rows] for i in range(3)], axis=-1)
        lhs = lhs.reshape(rows * width, 9 * chans)
        res = jnp.dot(lhs, weight[...], preferred_element_type=F32) + tshift
        res = res.reshape(rows, width, chans).astype(BF16)
        made[pl.ds(first, rows)] = res
        send(first).start()
        for r in range(rows):
            line = first + r
            ok = jnp.where((line >= 1) & (line <= bins), 1.0, 0.0).astype(F32)
            vals = res[r].astype(F32)[EDGE : EDGE + frames] * ok
            vals = vals.reshape(frames // 8, 8, chans)
            acc_s = acc_s + jnp.sum(vals, axis=0)
            acc_q = acc_q + jnp.sum(vals * vals, axis=0)
        return acc_s, acc_q

    def step(b, carry):
        first = b * rows
        window = act.at[pl.ds(first, 2 * rows + 2)]
        for r in range(rows):
            put_own(window.at[rows + 2 + r], jnp.minimum(first + rows + r, bins - 1))
        return matmul(window, first, *carry)

    zero = jnp.zeros((8, chans), F32)
    acc = lax.fori_loop(0, blocks - 1, step, (zero, zero))
    below = edges.shape[0] - 2
    put_edge(bins + 2, below, has_bottom)
    put_edge(bins + 3, below + 1, has_bottom)
    last = (blocks - 1) * rows
    acc_s, acc_q = matmul(act.at[pl.ds(last, rows + 2)], last, *acc)
    both = jnp.concatenate([jnp.sum(acc_s, axis=0, keepdims=True), jnp.sum(acc_q, axis=0, keepdims=True)], axis=0)
    moments[...] = jnp.broadcast_to(both[None], moments.shape)
    for i in range(blocks):
        send(i * rows).wait()


def mel_kernel(bins, frames, count, stats, small, source, folded, base, noisy, borders, mel, mel_in, sums, first_out, sems):
    chans = first_out.shape[-1]
    width = frames + 2 * EDGE
    lanes = sums.shape[1]
    parts = sems.shape[0]
    size = (bins + 2) // parts

    def fetch(i):
        part = pl.ds(i * size, size)
        return pltpu.make_async_copy(source.at[part], first_out.at[part], sems.at[i])

    for i in range(parts):
        fetch(i).start()
    scale, shift = norm_terms(stats[...], small[3:4], small[4:5], count)
    has_left, has_right = edge_flags("tm")
    has_top, has_bottom = edge_flags("freq")
    const = jnp.sum(small[5:6] * small[6:7], axis=1, keepdims=True)
    blank = jnp.zeros((5, chans), F32)
    taps = jnp.concatenate([folded[0], blank, folded[1], blank, folded[2], blank], axis=0)
    weights = jnp.concatenate([p for p in split3(taps)], axis=0)
    sums[...] = jnp.zeros_like(sums)
    group = 256 // width

    def rows(first, flags):
        vals = []
        for q in range(len(flags)):
            val = act_fn(first_out[first + q].astype(F32), scale, shift)
            val = jnp.concatenate(
                [val[:EDGE] * has_left, val[EDGE : EDGE + frames], val[EDGE + frames :] * has_right], axis=0
            )
            vals.append((val if flags[q] is None else val * flags[q]).astype(BF16))
        vals.append(jnp.zeros((256 - width * len(flags), chans), BF16))
        part = nt(weights, jnp.concatenate(vals, axis=0))
        part = part[0:24] + part[24:48] + part[48:72]
        for q in range(len(flags)):
            line = (part if q == 0 else pltpu.roll(part, 256 - q * width, 1))[:, :lanes]
            for i in range(3):
                at = (first + q + 2 - i) * 8
                at = at if isinstance(at, int) else pl.multiple_of(at, 8)
                sums[pl.ds(at, 8), :] += line[8 * i : 8 * i + 8]

    ready = 0
    at = 0
    while at < bins + 2:
        flags = [has_top if q == 0 else has_bottom if q == bins + 1 else None for q in range(at, min(at + group, bins + 2))]
        while ready * size < at + len(flags):
            fetch(ready).wait()
            ready += 1
        rows(at, flags)
        at += len(flags)
    t0 = sums[pl.ds(16, bins, stride=8), :]
    t1 = sums[pl.ds(17, bins, stride=8), :]
    t2 = sums[pl.ds(18, bins, stride=8), :]
    vel = pltpu.roll(t0, 1, 1) + t1 + pltpu.roll(t2, lanes - 1, 1) + base[...] + const

    fqs = lax.axis_size("freq")
    me = lax.axis_index("tm") * fqs + lax.axis_index("freq")
    before = borders[jnp.maximum(me - fqs, 0)][2:6, :bins].T
    behind = borders[jnp.minimum(me + fqs, borders.shape[0] - 1)][2:6, :bins].T
    blank = jnp.zeros((bins, 4), F32)
    old = [blank, before, noisy[...], behind, jnp.zeros((bins, lanes - frames - 12), F32)]
    old = jnp.concatenate(old, axis=1)
    res = old + STEP_SIZE * vel
    at = lax.broadcasted_iota(jnp.int32, (bins, lanes), 1) - EDGE
    pos = at + lax.axis_index("tm") * frames
    good = (at >= -4) & (at < frames + 4) & (pos >= 0) & (pos < frames * lax.axis_size("tm"))
    mel[...] = res[:, EDGE : EDGE + frames]
    mel_in[...] = jnp.where(good, res, 0.0).astype(BF16)


def up_kernel(frames, steps, paired, quarters, *refs):
    mels, refs = (refs[:2], refs[2:]) if paired else (refs[:1], refs[1:])
    pieces, refs = (refs[:4], refs[4:]) if quarters else (refs[:1], refs[1:])
    bias, source, vocal, fetched, wide, sems = refs
    tm, tms = lax.axis_index("tm"), lax.axis_size("tm")
    slabs = tms // steps
    taps = pieces[0].shape[1]
    high = frames + 8
    total, phases, outs = source.shape
    count = total // steps

    def fetch(step):
        return pltpu.make_async_copy(source.at[pl.ds(step * count, count)], fetched.at[step], sems.at[step])

    for step in range(steps):
        fetch(step).start()

    low = lax.axis_index("freq") == 0
    near = lax.axis_index("song") == 0
    if paired:
        a, b = mels[0][...], mels[1][...]
        mel = jnp.concatenate([jnp.where(low, a, b), jnp.where(low, b, a)], axis=0)
    else:
        mel = mels[0][...]
    melt = mel.astype(F32).T
    cols = jnp.concatenate([melt[4 + k : 4 + k + high].astype(BF16) for k in range(taps)], axis=1)
    line = lax.broadcasted_iota(jnp.int32, (high, 1), 0)
    pos = tm * frames + line - 1
    good = (pos >= 0) & (pos < frames * tms)

    def slab(at, k):
        if not quarters:
            return pieces[0][at, k]
        q = [p[at, k] for p in pieces]
        here = [jnp.where(near, q[0], q[1]), jnp.where(near, q[1], q[0])]
        there = [jnp.where(near, q[2], q[3]), jnp.where(near, q[3], q[2])]
        return jnp.concatenate(
            [jnp.where(low, h, t) for h, t in zip(here, there)] + [jnp.where(low, t, h) for h, t in zip(here, there)],
            axis=0,
        )

    shifted = []
    for step in range(steps):
        at = step * count
        rhs = [jnp.concatenate([slab(step * slabs + s, k) for k in range(taps)], axis=1) for s in range(slabs)]
        feats = nt(cols, jnp.concatenate(rhs, axis=0)) + bias[:, at : at + count]
        feats = jnp.where(good, feats, 0.0)
        shifted.append([feats[s : s + frames].astype(BF16) for s in range(3)])
    acc = [jnp.zeros((frames, outs), F32) for _ in range(4)]
    for step in range(steps):
        fetch(step).wait()
        for c in range(outs // 128):
            part = fetched[step, :, :, c * 128 : (c + 1) * 128]
            wide[step, c] = part.astype(F32).reshape(count * phases, 128)
        for k in range(phases):
            p = (k + 2) % 4
            s = 2 if k < 2 else (1 if k < 6 else 0)
            w = [wide.at[step, c][pl.ds(k, count, stride=phases), :] for c in range(outs // 128)]
            w = jnp.concatenate(w, axis=1).astype(BF16)
            acc[p] = acc[p] + jnp.dot(shifted[step][s], w, preferred_element_type=F32)
    size = 4 * frames
    rows = lax.broadcasted_iota(jnp.int32, (size, size), 0)
    place = lax.broadcasted_iota(jnp.int32, (size, size), 1)
    perm = jnp.where(rows % frames * 4 + rows // frames == place, 1.0, 0.0).astype(BF16)
    done = (jnp.concatenate(acc, axis=0) + bias[:, total:]).astype(BF16)
    res = lax.dot_general(done, perm, (((0,), (0,)), ((), ())), preferred_element_type=F32)
    vocal[...] = res.astype(BF16)


def exchange(sums):
    return lax.all_to_all(sums, ("tm", "freq"), 0, 0, tiled=True)


def neighbours(axis):
    n = lax.axis_size(axis)
    up = [(i, i + 1) for i in range(n - 1)]
    return up, [(j, i) for i, j in up]


def after(value, *others):
    return lax.optimization_barrier((value,) + others)[0]


def after(value, *others):
    return lax.optimization_barrier((value,) + others)[0]


def gather_slabs(weight, begin, middle, end):
    tms = lax.axis_size("tm")
    part = weight.shape[1] // 4
    index = lax.axis_index("freq") * 2 + lax.axis_index("song")
    own = after(lax.dynamic_slice_in_dim(weight, index * part, part, axis=1), *begin)
    swap = [(0, 1), (1, 0)]
    own = lax.all_to_all(jnp.broadcast_to(own[None], (tms,) + own.shape), "tm", 0, 0, tiled=True)
    own = after(own, *middle)
    far = lax.ppermute(own, "song", swap)
    other = lax.ppermute(own, "freq", swap)
    other_far = lax.ppermute(after(far, *end), "freq", swap)
    return [own, far, other, other_far]


def shards(
    latent,
    mel_noisy,
    time_shift,
    first_gain,
    first_shift,
    conv_first,
    second_gain,
    second_shift,
    conv_second,
    second_bias,
    out_proj,
    pre_weight,
    pre_bias,
    up_weight,
    up_bias,
):
    chans, bins, frames = latent.shape
    tms, fqs = lax.axis_size("tm"), lax.axis_size("freq")
    fq = lax.axis_index("freq")
    count = float(chans // GROUPS * bins * frames * tms * fqs)
    width = frames + 2 * EDGE
    lanes = -(-width // 128) * 128
    up, down = neighbours("tm")
    swap = [(0, 1), (1, 0)]
    x = jnp.transpose(latent, (1, 2, 0))

    devices = tms * fqs
    payload = jax.ShapeDtypeStruct((devices, 8, chans), F32)
    strip = jax.ShapeDtypeStruct((bins, EDGE, chans), BF16)
    sums, last, first = pl.pallas_call(
        sums_kernel, out_shape=(payload, strip, strip), in_specs=[VMEM] * 2, out_specs=(VMEM,) * 3, name="sums"
    )(x, mel_noisy)
    left = lax.ppermute(last, "tm", up)
    right = lax.ppermute(first, "tm", down)
    stats = exchange(sums)

    if fqs == 2:
        edge = jnp.concatenate([jnp.where(fq == 0, a[bins - 2 : bins], a[:2]) for a in (left, x, right)], axis=1)
        edges = lax.ppermute(edge, "freq", swap)
    else:
        fup, fdown = neighbours("freq")
        low = jnp.concatenate([a[:2] for a in (left, x, right)], axis=1)
        high = jnp.concatenate([a[bins - 2 : bins] for a in (left, x, right)], axis=1)
        edges = jnp.concatenate([lax.ppermute(high, "freq", fup), lax.ppermute(low, "freq", fdown)], axis=0)

    zero = jnp.zeros_like(out_proj)
    small = jnp.stack([first_gain, first_shift, time_shift, second_gain, second_shift, out_proj, second_bias, zero])
    rows = 6
    while (bins + 2) % rows:
        rows -= 1
    first_out, moments, base = pl.pallas_call(
        functools.partial(conv_kernel, bins, frames, rows, count),
        out_shape=(
            jax.ShapeDtypeStruct((bins + 2, width, chans), BF16),
            jax.ShapeDtypeStruct((devices, 2, chans), F32),
            jax.ShapeDtypeStruct((bins, lanes), F32),
        ),
        in_specs=[VMEM] * 7,
        out_specs=(pl.BlockSpec(memory_space=pl.ANY), VMEM, VMEM),
        scratch_shapes=[
            pltpu.VMEM((bins + 4 + rows, width, 3 * chans), BF16),
            pltpu.VMEM((bins + 2, width, chans), BF16),
            pltpu.SemaphoreType.DMA(((bins + 2) // rows,)),
        ],
        name="conv_first",
    )(stats, small, x, left, right, edges, conv_first.reshape(9 * chans, chans))
    stats2 = exchange(moments)

    folded = jnp.einsum("ijco,o->ijc", conv_second.astype(F32), out_proj, precision=lax.Precision.HIGHEST)
    mel_next, mel_in = pl.pallas_call(
        functools.partial(mel_kernel, bins, frames, count),
        out_shape=(jax.ShapeDtypeStruct((bins, frames), F32), jax.ShapeDtypeStruct((bins, lanes), BF16)),
        in_specs=[VMEM] * 2 + [pl.BlockSpec(memory_space=pl.ANY)] + [VMEM] * 4,
        out_specs=(VMEM,) * 2,
        scratch_shapes=[
            pltpu.VMEM(((bins + 4) * 8, lanes), F32),
            pltpu.VMEM((bins + 2, width, chans), BF16),
            pltpu.SemaphoreType.DMA(((bins + 2) // rows,)),
        ],
        name="mel",
    )(stats2, small, first_out, folded, base, mel_noisy, stats)

    depth = pre_weight.shape[0]
    total, phases, outs = up_weight.shape
    weight = jnp.transpose(pre_weight, (1, 0, 2))
    quarters = fqs == 2 and lax.axis_size("song") == 2 and depth % 64 == 0
    if quarters:
        pieces = gather_slabs(weight, (left, right), (moments,), (mel_in,))
    else:
        pieces = [after(lax.all_gather(weight, "tm", axis=0, tiled=False), mel_in)]
    slabs = 1
    while slabs * depth < 384 or tms % slabs:
        slabs += 1
    steps = tms // slabs
    if fqs == 2:
        mels = [mel_in, lax.ppermute(mel_in, "freq", swap)]
    else:
        mels = [lax.all_gather(mel_in, "freq", axis=0, tiled=True)]
    operands = mels + pieces + [jnp.concatenate([pre_bias, up_bias])[None]]
    vocal = pl.pallas_call(
        functools.partial(up_kernel, frames, steps, fqs == 2, quarters),
        out_shape=jax.ShapeDtypeStruct((outs, 4 * frames), BF16),
        in_specs=[VMEM] * len(operands) + [pl.BlockSpec(memory_space=pl.ANY)],
        out_specs=VMEM,
        scratch_shapes=[
            pltpu.VMEM((steps, total // steps, phases, outs), BF16),
            pltpu.VMEM((steps, outs // 128, total // steps * phases, 128), F32),
            pltpu.SemaphoreType.DMA((steps,)),
        ],
        name="up",
    )(*operands, up_weight)
    return (mel_next, vocal)


def solution(mesh):
    in_specs = (
        P(None, "freq", ("song", "tm")),
        P("freq", ("song", "tm")),
        P("song"),
        P(),
        P(),
        P(),
        P(),
        P(),
        P(),
        P(),
        P(),
        P("tm", None, None),
        P(),
        P(None, None, "freq"),
        P("freq"),
    )
    out_specs = (P("freq", ("song", "tm")), P("freq", ("song", "tm")))
    return jax.shard_map(shards, mesh=mesh, in_specs=in_specs, out_specs=out_specs, check_vma=False)
```

time: 245 us -> 82.7 us (0.34)
  matrix products: 76.5 us -> 1.04 us
  blocking collectives: 70.9 us -> 0 us
  local copies, waits for them, and re-layouts: 49.7 us -> 5.85 us
  Pallas kernels: 0 us -> 33.8 us
  other arithmetic: 14.3 us -> 0.91 us
  between operations: 14.5 us -> 1.12 us
  starting transfers between devices: 13.8 us -> 24.9 us
  waiting for transfers between devices: 4.92 us -> 14.6 us
    dot_general x33 -> x1, matrix products: 76.5 us -> 1.04 us  [shards(): jnp.einsum('ijco,o->ijc', conv_second.astype(F32), out_proj, precision=la...]
    psum x2 -> x0, blocking collectives: 68.3 us -> none  [group_moments(): first, second = lax.psum((first, second), ('tm', 'freq'))]
    slice x4 -> x0, local copies, waits for them, and re-layouts: 44.5 us -> none  [the longest x1 44.2 us: up_tap(): up_weight[:, k, :]]
    pallas_call x0 -> x4, Pallas kernels: none -> 33.8 us  [the longest x1 14.7 us: shards(): pl.pallas_call(functools.partial(conv_kernel, bins, frames, rows, count),...]
    all_to_all x0 -> x3, starting transfers between devices: none -> 15.9 us  [the longest x2 12.3 us: exchange(): return lax.all_to_all(sums, ('tm', 'freq'), 0, 0, tiled=True)]
    all_to_all x0 -> x3, waiting for transfers between devices: none -> 8.12 us  [the longest x2 8.01 us: exchange(): return lax.all_to_all(sums, ('tm', 'freq'), 0, 0, tiled=True)]
    convert_element_type x4 -> x0, other arithmetic: 5.9 us -> none  [the longest x2 4.49 us: norm_silu(): apply_norm(values_in, mean, scale_inv, gain, shift).astype(jnp.bfloat16)]
    concatenate x2, other arithmetic: 5.65 us -> 0.02 us  [the longest x1 0.01 us: shards(): jnp.concatenate([jnp.where(fq == 0, a[bins - 2:bins], a[:2]) for a in (le...]
  transfers between devices with their start and end apart: 11 -> 10, of which waited for: 3 -> 6; matrix products, arithmetic and copies ran while one was open for 49% -> 6% of each run, Pallas kernels for 0% -> 26%
where the time goes in v2:
time: 82.7 us; the launch traced here: 82.1 us
  Pallas kernels  33.8 us (41%)
  starting transfers between devices  24.9 us (30%)
  waiting for transfers between devices  14.6 us (18%)
  local copies, waits for them, and re-layouts  5.85 us (7%)
  between operations  1.12 us (1%)
  matrix products  1.04 us (1%)
  other arithmetic  0.91 us (1%)
    pallas_call x1, Pallas kernels, shards(): pl.pallas_call(functools.partial(conv_kernel, bins, frames, rows, count),...  14.7 us
    all_to_all x2, starting transfers between devices, exchange(): return lax.all_to_all(sums, ('tm', 'freq'), 0, 0, tiled=True)  12.3 us
    pallas_call x1, Pallas kernels, shards(): pl.pallas_call(functools.partial(up_kernel, frames, steps, fqs == 2, quar...  9.34 us
    all_to_all x2, waiting for transfers between devices, exchange(): return lax.all_to_all(sums, ('tm', 'freq'), 0, 0, tiled=True)  8.01 us
    pallas_call x1, Pallas kernels, shards(): pl.pallas_call(functools.partial(mel_kernel, bins, frames, count), out_sh...  6.73 us
    ppermute x1, starting transfers between devices, shards(): left = lax.ppermute(last, 'tm', up)  5.54 us
    ppermute x1, waiting for transfers between devices, shards(): left = lax.ppermute(last, 'tm', up)  3.84 us
    all_to_all x1, starting transfers between devices, gather_slabs(): lax.all_to_all(jnp.broadcast_to(own[None], (tms,) + own.shape), 'tm', 0,...  3.54 us
  transfers between devices with their start and end apart: 10, of which 6 were waited for; matrix products, arithmetic and copies ran while one was open for 6% of the time, Pallas kernels for 26%

profile of v2, /device:TPU:0, one launch (start us, length us, event | category | flops | bytes accessed | tf_op | source)
XLA Modules:
  0.0 82.1 jit_solution(1768812753836608635)
XLA Ops:
  0.6 0.0 copy-start
  0.6 3.0 %sums.1 = (f32[16,8,256]{2,1,0:T(8,128)}, bf16[64,8,256]{2,1,0:T(8,128)(2,1)}, bf16[64,8,256]{2,1,0:T(8,128)(2,1)}) custom-call(bf16[64,64,256]{2,1,0:T(8,128)(2,1)} %bitcast.19, f32[64,64]{1,0:T(8,128)} %noisy.3), custom_call_target="tpu_custom_call" | custom-call | tf_op jit(solution)/shard_map/sums/pallas_call | solution.py:385
  3.7 1.3 %collective-permute-start.1 = (bf16[64,8,256]{2,1,0:T(8,128)(2,1)}, bf16[64,8,256]{2,1,0:T(8,128)(2,1)S(1)}, u32[]{:S(2)}, u32[]{:S(2)}) collective-permute-start(bf16[64,8,256]{2,1,0:T(8,128)(2,1)} %get-tuple-element.15), channel_id=1, source_target_pairs={{2,0},{4,2},{6,4},{8,6},{10,8},{12,10},{14,12},{3,1},{5,3},{7,5},{... | collective-permute-start | bytes 786440 | tf_op jit(solution)/shard_map/ppermute | solution.py:389
  4.9 5.5 %collective-permute-start = (bf16[64,8,256]{2,1,0:T(8,128)(2,1)}, bf16[64,8,256]{2,1,0:T(8,128)(2,1)S(1)}, u32[]{:S(2)}, u32[]{:S(2)}) collective-permute-start(bf16[64,8,256]{2,1,0:T(8,128)(2,1)} %get-tuple-element.14), channel_id=1, source_target_pairs={{0,2},{2,4},{4,6},{6,8},{8,10},{10,12},{12,14},{1,3},{3,5},{5,7},{... | collective-permute-start | bytes 786440 | tf_op jit(solution)/shard_map/ppermute | solution.py:388
  10.5 6.3 %all-to-all-start = ((f32[16,8,256]{2,1,0:T(8,128)}), f32[16,8,256]{2,1,0:T(8,128)S(1)}, u32[]{:S(2)}, u32[]{:S(2)}) async-start(f32[16,8,256]{2,1,0:T(8,128)} %get-tuple-element.13), calls=%async_computation | async-start | bytes 262144 | tf_op jit(solution)/shard_map/all_to_all | solution.py:324
  16.8 0.9 %dynamic-slice_bitcast_fusion = bf16[7,48,128]{2,1,0:T(8,128)(2,1)S(1)} fusion(bf16[192,7,128]{2,0,1:T(8,128)(2,1)} %param.26, s32[]{:T(128)S(6)} %select_n.28), kind=kLoop, calls=%fused_computation | loop fusion | bytes 172036 | tf_op jit(solution)/shard_map/dynamic_slice | solution.py:345
  17.7 0.0 copy-start.11
  17.7 0.0 copy-start.13
  17.7 0.0 copy-start.14
  17.8 0.0 copy-start.15
  17.8 0.0 copy-start.16
  17.8 0.0 copy-start.17
  17.8 0.0 copy-start.18
  17.8 0.0 collective-permute-done.1.right
  17.8 0.0 copy-start.5
  17.8 3.8 %collective-permute-done.left = bf16[64,8,256]{2,1,0:T(8,128)(2,1)S(1)} collective-permute-done((bf16[64,8,256]{2,1,0:T(8,128)(2,1)}, bf16[64,8,256]{2,1,0:T(8,128)(2,1)S(1)}, u32[]{:S(2)}, u32[]{:S(2)}) %collective-permute-start) | collective-permute-done | bytes 262176 | tf_op jit(solution)/shard_map/ppermute | solution.py:388
  21.7 0.0 copy-start.6
  21.7 3.1 %all-to-all-done.stats.borders = f32[16,8,256]{2,1,0:T(8,128)S(1)} async-done(((f32[16,8,256]{2,1,0:T(8,128)}), f32[16,8,256]{2,1,0:T(8,128)S(1)}, u32[]{:S(2)}, u32[]{:S(2)}) %all-to-all-start) | async-done | bytes 131104 | tf_op jit(solution)/shard_map/all_to_all | solution.py:324
  24.7 0.0 copy-start.2
  24.7 0.9 %broadcast_in_dim.4 = bf16[8,7,48,128]{3,2,1,0:T(8,128)(2,1)} broadcast(bf16[7,48,128]{2,1,0:T(8,128)(2,1)S(1)} %dynamic-slice_bitcast_fusion), dimensions={1,2,3} | broadcast | bytes 774144 | tf_op jit(solution)/shard_map/broadcast_in_dim | solution.py:347
  25.7 3.5 %all-to-all-start.2 = ((bf16[8,7,48,128]{3,2,1,0:T(8,128)(2,1)}), bf16[8,7,48,128]{3,2,1,0:T(8,128)(2,1)S(1)}, u32[]{:S(2)}, u32[]{:S(2)}) async-start(bf16[8,7,48,128]{3,2,1,0:T(8,128)(2,1)} %broadcast_in_dim.4), calls=%async_computation.2 | async-start | bytes 1376256 | tf_op jit(solution)/shard_map/all_to_all | solution.py:347
  29.2 0.9 %slice_select_fusion = bf16[2,64,256]{2,1,0:T(8,128)(2,1)S(1)} fusion(bf16[64,64,256]{2,1,0:T(8,128)(2,1)} %bitcast.20, pred[]{:T(512)S(6)} %eq.2), kind=kLoop, calls=%fused_computation.2 | loop fusion | flops 32768 | bytes 196609 | tf_op jit(solution)/shard_map/jit(_where)/select_n | solution.py:393
  30.1 0.0 copy-done.5
  30.1 0.0 copy-done.6
  30.1 0.0 copy-done.2
  30.2 0.1 collective-permute-start.2
  30.3 0.0 copy-done.11
  30.3 0.0 copy-done.13
  30.3 0.0 copy-done.14
  30.3 0.0 copy-done.15
  30.3 0.0 copy-done.16
  30.3 0.0 copy-done.17
  30.3 0.0 copy-done.18
  30.3 0.6 stack.31.small
  30.9 0.6 collective-permute-done.2.edges
  31.5 0.0 copy-start.8
  31.5 0.6 copy-done.8
  32.1 14.7 %conv_first.1 = (bf16[66,80,256]{2,1,0:T(8,128)(2,1)}, f32[16,2,256]{2,1,0:T(2,128)}, f32[64,128]{1,0:T(8,128)}) custom-call(f32[16,8,256]{2,1,0:T(8,128)} %copy-done.2, f32[8,256]{1,0:T(8,128)} %stack.31.small, bf16[64,64,256]{2,1,0:T(8,128)(2,1)} %bitcast.21, bf16[64,8,256]{2,1,0:T(8,128)(2,1)} %copy-done.6, bf16[64,8,256]{2,1,0:T(8,128)(2,1)} %copy-done.5, ...), custom_call_target="tpu_custom_call" | custom-call | tf_op jit(solution)/shard_map/conv_first/pallas_call | solution.py:406
  46.8 0.1 all-to-all-done.2.refs_2_
  47.0 0.0 copy-start.1
  47.0 1.5 %collective-permute-start.4 = (bf16[8,7,48,128]{3,2,1,0:T(8,128)(2,1)S(1)}, bf16[8,7,48,128]{3,2,1,0:T(8,128)(2,1)S(1)}, u32[]{:S(2)}, u32[]{:S(2)}) collective-permute-start(bf16[8,7,48,128]{3,2,1,0:T(8,128)(2,1)S(1)} %all-to-all-done.2.refs_2_), channel_id=1, source_target_pairs={{0,16},{16,0},{1,17},{17,1},{2,18},{18,2},{3,19},{19,3},{4,20},{20... | collective-permute-start | bytes 2064392 | tf_op jit(solution)/shard_map/ppermute | solution.py:349
  48.5 6.0 %all-to-all-start.1 = ((f32[16,2,256]{2,1,0:T(2,128)}), f32[16,2,256]{2,1,0:T(2,128)S(1)}, u32[]{:S(2)}, u32[]{:S(2)}) async-start(f32[16,2,256]{2,1,0:T(2,128)} %get-tuple-element.16), calls=%async_computation.1 | async-start | bytes 65536 | tf_op jit(solution)/shard_map/all_to_all | solution.py:324
  54.5 0.0 copy-done
  54.5 1.0 %fusion = f32[1,3,3,256]{3,0,2,1:T(1,128)S(1)} fusion(bf16[3,3,256,256]{3,2,1,0:T(8,128)(2,1)S(1)} %copy-done, f32[256,1,1,1]{0,1,3,2:T(1,128)S(1)} %bitcast.25), kind=kOutput, calls=%fused_computation.7 | convolution fusion | flops 7077888 | bytes 1189888 | tf_op jit(solution)/shard_map/ijco,o->ijc/dot_general | solution.py:424
  55.5 0.6 copy.20
  56.1 5.0 %all-to-all-done.1.stats = f32[16,2,256]{2,1,0:T(2,128)S(1)} async-done(((f32[16,2,256]{2,1,0:T(2,128)}), f32[16,2,256]{2,1,0:T(2,128)S(1)}, u32[]{:S(2)}, u32[]{:S(2)}) %all-to-all-start.1) | async-done | bytes 32800 | tf_op jit(solution)/shard_map/all_to_all | solution.py:324
  61.1 0.6 copy-done.7
  61.7 6.7 %mel.1 = (f32[64,64]{1,0:T(8,128)}, bf16[64,128]{1,0:T(8,128)(2,1)}) custom-call(f32[16,2,256]{2,1,0:T(2,128)} %copy-done.7, f32[8,256]{1,0:T(8,128)} %stack.31.small, bf16[66,80,256]{2,1,0:T(8,128)(2,1)} %get-tuple-element.17.source, f32[3,3,256]{2,1,0:T(4,128)} %bitcast.23, f32[64,128]{1,0:T(8,128)} %get-tuple-element.18.base, f32[64,64]{1,0:T(8,128)} %noisy.3, ...), custom_call_target="tpu_custom_call" | custom-call | tf_op jit(solution)/shard_map/mel/pallas_call | solution.py:425
  68.4 0.0 copy-done.1
  68.4 0.1 collective-permute-start.5
  68.5 0.0 collective-permute-done.4.refs_3_
  68.5 0.0 copy-start.3
  68.5 0.5 collective-permute-start.6
  69.0 0.1 collective-permute-start.3
  69.1 0.0 copy-done.10
  69.1 0.0 copy-done.12
  69.1 0.6 broadcast_in_dim.10.refs_6_
  69.7 2.0 %collective-permute-done.3.refs_1_ = bf16[64,128]{1,0:T(8,128)(2,1)S(1)} collective-permute-done((bf16[64,128]{1,0:T(8,128)(2,1)}, bf16[64,128]{1,0:T(8,128)(2,1)S(1)}, u32[]{:S(2)}, u32[]{:S(2)}) %collective-permute-start.3) | collective-permute-done | bytes 16416 | tf_op jit(solution)/shard_map/ppermute | solution.py:451
  71.8 0.0 collective-permute-done.5.refs_4_
  71.8 0.0 collective-permute-done.6.refs_5_
  71.8 0.0 copy-done.3
  71.8 0.6 copy-done.9
  72.4 0.3 copy-done.4
  72.6 9.3 %up.1 = bf16[384,256]{1,0:T(8,128)(2,1)} custom-call(bf16[64,128]{1,0:T(8,128)(2,1)} %get-tuple-element.20.refs_0_, bf16[64,128]{1,0:T(8,128)(2,1)} %copy-done.9, bf16[8,7,48,128]{3,2,1,0:T(8,128)(2,1)} %copy-done.1, bf16[8,7,48,128]{3,2,1,0:T(8,128)(2,1)} %copy-done.3, bf16[8,7,48,128]{3,2,1,0:T(8,128)(2,1)} %copy-done.4, ...), custom_call_target="tpu_custom_call" | custom-call | tf_op jit(solution)/shard_map/up/pallas_call | solution.py:455
  (10 shorter events, 0.0 us)
Async XLA Ops:
  0.6 53.8 %copy-start = (bf16[3,3,256,256]{3,2,1,0:T(8,128)(2,1)S(1)}, bf16[3,3,256,256]{3,2,1,0:T(8,128)(2,1)}, u32[]{:S(2)}) copy-start(bf16[3,3,256,256]{3,2,1,0:T(8,128)(2,1)} %param.23) | copy-start | bytes 3538948
  3.7 14.2 %collective-permute-start.1 = (bf16[64,8,256]{2,1,0:T(8,128)(2,1)}, bf16[64,8,256]{2,1,0:T(8,128)(2,1)S(1)}, u32[]{:S(2)}, u32[]{:S(2)}) collective-permute-start(bf16[64,8,256]{2,1,0:T(8,128)(2,1)} %get-tuple-element.15), channel_id=1, source_target_pairs={{2,0},{4,2},{6,4},{8,6},{10,8},{12,10},{14,12},{3,1},{5,3},{7,5},{... | collective-permute-start | bytes 786440 | tf_op jit(solution)/shard_map/ppermute | solution.py:389
  4.9 16.7 %collective-permute-start = (bf16[64,8,256]{2,1,0:T(8,128)(2,1)}, bf16[64,8,256]{2,1,0:T(8,128)(2,1)S(1)}, u32[]{:S(2)}, u32[]{:S(2)}) collective-permute-start(bf16[64,8,256]{2,1,0:T(8,128)(2,1)} %get-tuple-element.14), channel_id=1, source_target_pairs={{0,2},{2,4},{4,6},{6,8},{8,10},{10,12},{12,14},{1,3},{3,5},{5,7},{... | collective-permute-start | bytes 786440 | tf_op jit(solution)/shard_map/ppermute | solution.py:388
  10.5 14.2 %all-to-all-start = ((f32[16,8,256]{2,1,0:T(8,128)}), f32[16,8,256]{2,1,0:T(8,128)S(1)}, u32[]{:S(2)}, u32[]{:S(2)}) async-start(f32[16,8,256]{2,1,0:T(8,128)} %get-tuple-element.13), calls=%async_computation | async-start | bytes 262144 | tf_op jit(solution)/shard_map/all_to_all | solution.py:324
  17.7 12.5 %copy-start.11 = (f32[256]{0:T(256)S(1)}, f32[256]{0:T(256)}, u32[]{:S(2)}) copy-start(f32[256]{0:T(256)} %param.25) | copy-start | bytes 3076
  17.7 12.5 %copy-start.13 = (f32[256]{0:T(256)S(1)}, f32[256]{0:T(256)}, u32[]{:S(2)}) copy-start(f32[256]{0:T(256)} %param.18) | copy-start | bytes 3076
  17.7 12.5 %copy-start.14 = (f32[256]{0:T(256)S(1)}, f32[256]{0:T(256)}, u32[]{:S(2)}) copy-start(f32[256]{0:T(256)} %param.19) | copy-start | bytes 3076
  17.8 12.5 %copy-start.15 = (f32[256]{0:T(256)S(1)}, f32[256]{0:T(256)}, u32[]{:S(2)}) copy-start(f32[256]{0:T(256)} %param.17) | copy-start | bytes 3076
  17.8 12.5 %copy-start.16 = (f32[256]{0:T(256)S(1)}, f32[256]{0:T(256)}, u32[]{:S(2)}) copy-start(f32[256]{0:T(256)} %param.21) | copy-start | bytes 3076
  17.8 12.5 %copy-start.17 = (f32[256]{0:T(256)S(1)}, f32[256]{0:T(256)}, u32[]{:S(2)}) copy-start(f32[256]{0:T(256)} %param.22) | copy-start | bytes 3076
  17.8 12.5 %copy-start.18 = (f32[256]{0:T(256)S(1)}, f32[256]{0:T(256)}, u32[]{:S(2)}) copy-start(f32[256]{0:T(256)} %param.24) | copy-start | bytes 3076
  17.8 12.3 %copy-start.5 = (bf16[64,8,256]{2,1,0:T(8,128)(2,1)}, bf16[64,8,256]{2,1,0:T(8,128)(2,1)S(1)}, u32[]{:S(2)}) copy-start(bf16[64,8,256]{2,1,0:T(8,128)(2,1)S(1)} %collective-permute-done.1.right) | copy-start | bytes 786436
  21.7 8.5 %copy-start.6 = (bf16[64,8,256]{2,1,0:T(8,128)(2,1)}, bf16[64,8,256]{2,1,0:T(8,128)(2,1)S(1)}, u32[]{:S(2)}) copy-start(bf16[64,8,256]{2,1,0:T(8,128)(2,1)S(1)} %collective-permute-done.left) | copy-start | bytes 786436
  24.7 5.4 %copy-start.2 = (f32[16,8,256]{2,1,0:T(8,128)}, f32[16,8,256]{2,1,0:T(8,128)S(1)}, u32[]{:S(2)}) copy-start(f32[16,8,256]{2,1,0:T(8,128)S(1)} %all-to-all-done.stats.borders) | copy-start | bytes 393220
  25.7 21.3 %all-to-all-start.2 = ((bf16[8,7,48,128]{3,2,1,0:T(8,128)(2,1)}), bf16[8,7,48,128]{3,2,1,0:T(8,128)(2,1)S(1)}, u32[]{:S(2)}, u32[]{:S(2)}) async-start(bf16[8,7,48,128]{3,2,1,0:T(8,128)(2,1)} %broadcast_in_dim.4), calls=%async_computation.2 | async-start | bytes 1376256 | tf_op jit(solution)/shard_map/all_to_all | solution.py:347
  30.2 1.3 %collective-permute-start.2 = (bf16[2,80,256]{2,1,0:T(8,128)(2,1)S(1)}, bf16[2,80,256]{2,1,0:T(8,128)(2,1)S(1)}, u32[]{:S(2)}, u32[]{:S(2)}) collective-permute-start(bf16[2,80,256]{2,1,0:T(8,128)(2,1)S(1)} %pad_maximum_fusion), channel_id=1, source_target_pairs={{0,1},{1,0},{2,3},{3,2},{4,5},{5,4},{6,7},{7,6},{8,9},{9,8},{10,11... | collective-permute-start | bytes 245768 | tf_op jit(solution)/shard_map/ppermute | solution.py:394
  31.5 0.6 copy-start.8
  47.0 21.5 %copy-start.1 = (bf16[8,7,48,128]{3,2,1,0:T(8,128)(2,1)}, bf16[8,7,48,128]{3,2,1,0:T(8,128)(2,1)S(1)}, u32[]{:S(2)}) copy-start(bf16[8,7,48,128]{3,2,1,0:T(8,128)(2,1)S(1)} %all-to-all-done.2.refs_2_) | copy-start | bytes 2064388
  47.0 21.6 %collective-permute-start.4 = (bf16[8,7,48,128]{3,2,1,0:T(8,128)(2,1)S(1)}, bf16[8,7,48,128]{3,2,1,0:T(8,128)(2,1)S(1)}, u32[]{:S(2)}, u32[]{:S(2)}) collective-permute-start(bf16[8,7,48,128]{3,2,1,0:T(8,128)(2,1)S(1)} %all-to-all-done.2.refs_2_), channel_id=1, source_target_pairs={{0,16},{16,0},{1,17},{17,1},{2,18},{18,2},{3,19},{19,3},{4,20},{20... | collective-permute-start | bytes 2064392 | tf_op jit(solution)/shard_map/ppermute | solution.py:349
  48.5 12.6 %all-to-all-start.1 = ((f32[16,2,256]{2,1,0:T(2,128)}), f32[16,2,256]{2,1,0:T(2,128)S(1)}, u32[]{:S(2)}, u32[]{:S(2)}) async-start(f32[16,2,256]{2,1,0:T(2,128)} %get-tuple-element.16), calls=%async_computation.1 | async-start | bytes 65536 | tf_op jit(solution)/shard_map/all_to_all | solution.py:324
  61.1 0.6 copy-start.7
  61.7 7.4 %copy-start.10 = (f32[1536]{0:T(1024)S(1)}, f32[1536]{0:T(1024)}, u32[]{:S(2)}) copy-start(f32[1536]{0:T(1024)} %param.27) | copy-start | bytes 18436
  61.7 7.4 %copy-start.12 = (f32[384]{0:T(512)S(1)}, f32[384]{0:T(512)}, u32[]{:S(2)}) copy-start(f32[384]{0:T(512)} %param.29) | copy-start | bytes 4612
  68.4 3.3 %collective-permute-start.5 = (bf16[8,7,48,128]{3,2,1,0:T(8,128)(2,1)S(1)}, bf16[8,7,48,128]{3,2,1,0:T(8,128)(2,1)S(1)}, u32[]{:S(2)}, u32[]{:S(2)}) collective-permute-start(bf16[8,7,48,128]{3,2,1,0:T(8,128)(2,1)S(1)} %all-to-all-done.2.refs_2_), channel_id=1, source_target_pairs={{0,1},{1,0},{2,3},{3,2},{4,5},{5,4},{6,7},{7,6},{8,9},{9,8},{10,11... | collective-permute-start | bytes 2064392 | tf_op jit(solution)/shard_map/ppermute | solution.py:350
  68.5 3.3 %copy-start.3 = (bf16[8,7,48,128]{3,2,1,0:T(8,128)(2,1)}, bf16[8,7,48,128]{3,2,1,0:T(8,128)(2,1)S(1)}, u32[]{:S(2)}) copy-start(bf16[8,7,48,128]{3,2,1,0:T(8,128)(2,1)S(1)} %collective-permute-done.4.refs_3_) | copy-start | bytes 2064388
  68.5 3.2 %collective-permute-start.6 = (bf16[8,7,48,128]{3,2,1,0:T(8,128)(2,1)S(1)}, bf16[8,7,48,128]{3,2,1,0:T(8,128)(2,1)}, u32[]{:S(2)}, u32[]{:S(2)}) collective-permute-start(bf16[8,7,48,128]{3,2,1,0:T(8,128)(2,1)S(1)} %collective-permute-done.4.refs_3_), channel_id=1, source_target_pairs={{0,1},{1,0},{2,3},{3,2},{4,5},{5,4},{6,7},{7,6},{8,9},{9,8},{10,11... | collective-permute-start | bytes 2064392 | tf_op jit(solution)/shard_map/ppermute | solution.py:351
  69.0 2.7 %collective-permute-start.3 = (bf16[64,128]{1,0:T(8,128)(2,1)}, bf16[64,128]{1,0:T(8,128)(2,1)S(1)}, u32[]{:S(2)}, u32[]{:S(2)}) collective-permute-start(bf16[64,128]{1,0:T(8,128)(2,1)} %get-tuple-element.20.refs_0_), channel_id=1, source_target_pairs={{0,1},{1,0},{2,3},{3,2},{4,5},{5,4},{6,7},{7,6},{8,9},{9,8},{10,11... | collective-permute-start | bytes 49160 | tf_op jit(solution)/shard_map/ppermute | solution.py:451
  71.8 0.6 copy-start.9
  71.8 0.9 %copy-start.4 = (bf16[8,7,48,128]{3,2,1,0:T(8,128)(2,1)}, bf16[8,7,48,128]{3,2,1,0:T(8,128)(2,1)S(1)}, u32[]{:S(2)}) copy-start(bf16[8,7,48,128]{3,2,1,0:T(8,128)(2,1)S(1)} %collective-permute-done.5.refs_4_) | copy-start | bytes 2064388

commit v3 on v2

--- a/solution.py
+++ b/solution.py
@@ -254,25 +254,36 @@
 def up_kernel(frames, steps, paired, quarters, *refs):
     mels, refs = (refs[:2], refs[2:]) if paired else (refs[:1], refs[1:])
     pieces, refs = (refs[:4], refs[4:]) if quarters else (refs[:1], refs[1:])
-    bias, source, vocal, fetched, wide, sems = refs
+    bias, final, source, vocal, fetched, wide, sems = refs
     tm, tms = lax.axis_index("tm"), lax.axis_size("tm")
-    slabs = tms // steps
-    taps = pieces[0].shape[1]
+    slabs, taps, depth, _ = pieces[0].shape
     high = frames + 8
     total, phases, outs = source.shape
+    steps = 4 if quarters else steps
     count = total // steps
+    fq, song = lax.axis_index("freq"), lax.axis_index("song")
+    places = [fq * 2 + song, fq * 2 + 1 - song, 2 - fq * 2 + song, 3 - fq * 2 - song] if quarters else None
 
     def fetch(step):
-        return pltpu.make_async_copy(source.at[pl.ds(step * count, count)], fetched.at[step], sems.at[step])
+        if not quarters:
+            at = pl.ds(step * count, count)
+            return [pltpu.make_async_copy(source.at[at], fetched.at[step], sems.at[step, 0])]
+        return [
+            pltpu.make_async_copy(
+                source.at[pl.ds(s * 4 * depth + places[step] * depth, depth)],
+                fetched.at[step, pl.ds(s * depth, depth)],
+                sems.at[step, s],
+            )
+            for s in range(slabs)
+        ]
 
     for step in range(steps):
-        fetch(step).start()
-
-    low = lax.axis_index("freq") == 0
-    near = lax.axis_index("song") == 0
+        for copy in fetch(step):
+            copy.start()
+
     if paired:
         a, b = mels[0][...], mels[1][...]
-        mel = jnp.concatenate([jnp.where(low, a, b), jnp.where(low, b, a)], axis=0)
+        mel = jnp.concatenate([jnp.where(fq == 0, a, b), jnp.where(fq == 0, b, a)], axis=0)
     else:
         mel = mels[0][...]
     melt = mel.astype(F32).T
@@ -281,27 +292,17 @@
     pos = tm * frames + line - 1
     good = (pos >= 0) & (pos < frames * tms)
 
-    def slab(at, k):
-        if not quarters:
-            return pieces[0][at, k]
-        q = [p[at, k] for p in pieces]
-        here = [jnp.where(near, q[0], q[1]), jnp.where(near, q[1], q[0])]
-        there = [jnp.where(near, q[2], q[3]), jnp.where(near, q[3], q[2])]
-        return jnp.concatenate(
-            [jnp.where(low, h, t) for h, t in zip(here, there)] + [jnp.where(low, t, h) for h, t in zip(here, there)],
-            axis=0,
-        )
-
     shifted = []
     for step in range(steps):
-        at = step * count
-        rhs = [jnp.concatenate([slab(step * slabs + s, k) for k in range(taps)], axis=1) for s in range(slabs)]
-        feats = nt(cols, jnp.concatenate(rhs, axis=0)) + bias[:, at : at + count]
+        piece, per = (pieces[step], range(slabs)) if quarters else (pieces[0], range(step * slabs // steps, (step + 1) * slabs // steps))
+        rhs = [jnp.concatenate([piece[s, k] for k in range(taps)], axis=1) for s in per]
+        feats = nt(cols, jnp.concatenate(rhs, axis=0)) + bias[places[step] if quarters else step]
         feats = jnp.where(good, feats, 0.0)
         shifted.append([feats[s : s + frames].astype(BF16) for s in range(3)])
     acc = [jnp.zeros((frames, outs), F32) for _ in range(4)]
     for step in range(steps):
-        fetch(step).wait()
+        for copy in fetch(step):
+            copy.wait()
         for c in range(outs // 128):
             part = fetched[step, :, :, c * 128 : (c + 1) * 128]
             wide[step, c] = part.astype(F32).reshape(count * phases, 128)
@@ -315,7 +316,7 @@
     rows = lax.broadcasted_iota(jnp.int32, (size, size), 0)
     place = lax.broadcasted_iota(jnp.int32, (size, size), 1)
     perm = jnp.where(rows % frames * 4 + rows // frames == place, 1.0, 0.0).astype(BF16)
-    done = (jnp.concatenate(acc, axis=0) + bias[:, total:]).astype(BF16)
+    done = (jnp.concatenate(acc, axis=0) + final[...]).astype(BF16)
     res = lax.dot_general(done, perm, (((0,), (0,)), ((), ())), preferred_element_type=F32)
     vocal[...] = res.astype(BF16)
 
@@ -400,7 +401,7 @@
 
     zero = jnp.zeros_like(out_proj)
     small = jnp.stack([first_gain, first_shift, time_shift, second_gain, second_shift, out_proj, second_bias, zero])
-    rows = 6
+    rows = 11
     while (bins + 2) % rows:
         rows -= 1
     first_out, moments, base = pl.pallas_call(
@@ -421,6 +422,9 @@
     )(stats, small, x, left, right, edges, conv_first.reshape(9 * chans, chans))
     stats2 = exchange(moments)
 
+    parts = 2
+    while (bins + 2) % parts:
+        parts -= 1
     folded = jnp.einsum("ijco,o->ijc", conv_second.astype(F32), out_proj, precision=lax.Precision.HIGHEST)
     mel_next, mel_in = pl.pallas_call(
         functools.partial(mel_kernel, bins, frames, count),
@@ -430,7 +434,7 @@
         scratch_shapes=[
             pltpu.VMEM(((bins + 4) * 8, lanes), F32),
             pltpu.VMEM((bins + 2, width, chans), BF16),
-            pltpu.SemaphoreType.DMA(((bins + 2) // rows,)),
+            pltpu.SemaphoreType.DMA((parts,)),
         ],
         name="mel",
     )(stats2, small, first_out, folded, base, mel_noisy, stats)
@@ -440,7 +444,7 @@
     weight = jnp.transpose(pre_weight, (1, 0, 2))
     quarters = fqs == 2 and lax.axis_size("song") == 2 and depth % 64 == 0
     if quarters:
-        pieces = gather_slabs(weight, (left, right), (moments,), (mel_in,))
+        pieces = gather_slabs(weight, (right,), (moments,), (mel_in,))
     else:
         pieces = [after(lax.all_gather(weight, "tm", axis=0, tiled=False), mel_in)]
     slabs = 1
@@ -451,7 +455,12 @@
         mels = [mel_in, lax.ppermute(mel_in, "freq", swap)]
     else:
         mels = [lax.all_gather(mel_in, "freq", axis=0, tiled=True)]
-    operands = mels + pieces + [jnp.concatenate([pre_bias, up_bias])[None]]
+    if quarters:
+        steps = 4
+        bias = pre_bias.reshape(tms, 4, depth // 4).swapaxes(0, 1).reshape(4, 1, total // 4)
+    else:
+        bias = pre_bias.reshape(steps, 1, total // steps)
+    operands = mels + pieces + [bias, up_bias[None]]
     vocal = pl.pallas_call(
         functools.partial(up_kernel, frames, steps, fqs == 2, quarters),
         out_shape=jax.ShapeDtypeStruct((outs, 4 * frames), BF16),
@@ -460,7 +469,7 @@
         scratch_shapes=[
             pltpu.VMEM((steps, total // steps, phases, outs), BF16),
             pltpu.VMEM((steps, outs // 128, total // steps * phases, 128), F32),
-            pltpu.SemaphoreType.DMA((steps,)),
+            pltpu.SemaphoreType.DMA((steps, tms if quarters else 1)),
         ],
         name="up",
     )(*operands, up_weight)

time: 82.7 us -> 96.7 us (1.17)
  starting transfers between devices: 24.9 us -> 33.5 us
  waiting for transfers between devices: 14.6 us -> 21 us
  Pallas kernels: 33.8 us -> 32 us
    all_to_all x2, starting transfers between devices: 12.3 us -> 22.6 us  [exchange(): return lax.all_to_all(sums, ('tm', 'freq'), 0, 0, tiled=True)]
    ppermute x1, waiting for transfers between devices: 3.84 us -> 7.36 us  [shards(): left = lax.ppermute(last, 'tm', up)]
    all_to_all x2, waiting for transfers between devices: 8.01 us -> 11.3 us  [exchange(): return lax.all_to_all(sums, ('tm', 'freq'), 0, 0, tiled=True)]
    pallas_call x1, Pallas kernels: 6.73 us -> 4.96 us  [shards(): pl.pallas_call(functools.partial(mel_kernel, bins, frames, count), out_sh...]
    ppermute x1, starting transfers between devices: 5.54 us -> 3.82 us  [shards(): left = lax.ppermute(last, 'tm', up)]
    unnamed x38 -> x40, local copies, waits for them, and re-layouts: 2.17 us -> 2.19 us
  transfers between devices with their start and end apart: 10 -> 10, of which waited for: 6 -> 6; matrix products, arithmetic and copies ran while one was open for 6% -> 6% of each run, Pallas kernels for 26% -> 20%
where the time goes in v3:
time: 96.7 us; the launch traced here: 96.2 us
  starting transfers between devices  33.5 us (35%)
  Pallas kernels  32 us (33%)
  waiting for transfers between devices  21 us (22%)
  local copies, waits for them, and re-layouts  6.68 us (7%)
  between operations  1.12 us (1%)
  matrix products  1.04 us (1%)
    all_to_all x2, starting transfers between devices, exchange(): return lax.all_to_all(sums, ('tm', 'freq'), 0, 0, tiled=True)  22.6 us
    pallas_call x1, Pallas kernels, shards(): pl.pallas_call(functools.partial(conv_kernel, bins, frames, rows, count),...  14.1 us
    all_to_all x2, waiting for transfers between devices, exchange(): return lax.all_to_all(sums, ('tm', 'freq'), 0, 0, tiled=True)  11.3 us
    pallas_call x1, Pallas kernels, shards(): pl.pallas_call(functools.partial(up_kernel, frames, steps, fqs == 2, quar...  9.93 us
    ppermute x1, waiting for transfers between devices, shards(): left = lax.ppermute(last, 'tm', up)  7.36 us
    pallas_call x1, Pallas kernels, shards(): pl.pallas_call(functools.partial(mel_kernel, bins, frames, count), out_sh...  4.96 us
    ppermute x1, starting transfers between devices, shards(): left = lax.ppermute(last, 'tm', up)  3.82 us
    all_to_all x1, starting transfers between devices, gather_slabs(): lax.all_to_all(jnp.broadcast_to(own[None], (tms,) + own.shape), 'tm', 0,...  3.54 us
  transfers between devices with their start and end apart: 10, of which 6 were waited for; matrix products, arithmetic and copies ran while one was open for 6% of the time, Pallas kernels for 20%

profile of v3, /device:TPU:0, one launch (start us, length us, event | category | flops | bytes accessed | tf_op | source)
XLA Modules:
  0.0 96.2 jit_solution(1483274183427446614)
XLA Ops:
  0.6 0.0 copy-start
  0.6 3.0 %sums.1 = (f32[16,8,256]{2,1,0:T(8,128)}, bf16[64,8,256]{2,1,0:T(8,128)(2,1)}, bf16[64,8,256]{2,1,0:T(8,128)(2,1)}) custom-call(bf16[64,64,256]{2,1,0:T(8,128)(2,1)} %bitcast.20, f32[64,64]{1,0:T(8,128)} %noisy.3), custom_call_target="tpu_custom_call" | custom-call | tf_op jit(solution)/shard_map/sums/pallas_call | solution.py:386
  3.7 1.3 %collective-permute-start.1 = (bf16[64,8,256]{2,1,0:T(8,128)(2,1)}, bf16[64,8,256]{2,1,0:T(8,128)(2,1)S(1)}, u32[]{:S(2)}, u32[]{:S(2)}) collective-permute-start(bf16[64,8,256]{2,1,0:T(8,128)(2,1)} %get-tuple-element.15), channel_id=1, source_target_pairs={{2,0},{4,2},{6,4},{8,6},{10,8},{12,10},{14,12},{3,1},{5,3},{7,5},{... | collective-permute-start | bytes 786440 | tf_op jit(solution)/shard_map/ppermute | solution.py:390
  4.9 8.6 %all-to-all-start = ((f32[16,8,256]{2,1,0:T(8,128)}), f32[16,8,256]{2,1,0:T(8,128)S(1)}, u32[]{:S(2)}, u32[]{:S(2)}) async-start(f32[16,8,256]{2,1,0:T(8,128)} %get-tuple-element.13), calls=%async_computation | async-start | bytes 262144 | tf_op jit(solution)/shard_map/all_to_all | solution.py:325
  13.5 0.0 copy-start.19
  13.5 0.9 dynamic-slice_bitcast_fusion
  14.5 0.0 copy-start.11
  14.5 0.0 copy-start.13
  14.5 0.0 copy-start.14
  14.5 0.0 copy-start.15
  14.5 0.0 copy-start.16
  14.5 0.0 copy-start.17
  14.5 0.0 copy-start.18
  14.5 0.5 collective-permute-done.1.right
  15.1 6.4 %all-to-all-done.stats.borders = f32[16,8,256]{2,1,0:T(8,128)S(1)} async-done(((f32[16,8,256]{2,1,0:T(8,128)}), f32[16,8,256]{2,1,0:T(8,128)S(1)}, u32[]{:S(2)}, u32[]{:S(2)}) %all-to-all-start) | async-done | bytes 131104 | tf_op jit(solution)/shard_map/all_to_all | solution.py:325
  21.4 0.9 broadcast_in_dim.4
  22.3 3.5 %all-to-all-start.2 = ((bf16[8,7,48,128]{3,2,1,0:T(8,128)(2,1)}), bf16[8,7,48,128]{3,2,1,0:T(8,128)(2,1)S(1)}, u32[]{:S(2)}, u32[]{:S(2)}) async-start(bf16[8,7,48,128]{3,2,1,0:T(8,128)(2,1)} %broadcast_in_dim.4), calls=%async_computation.2 | async-start | bytes 1376256 | tf_op jit(solution)/shard_map/all_to_all | solution.py:348
  25.9 0.0 copy-done.19
  25.9 3.8 %collective-permute-start = (bf16[64,8,256]{2,1,0:T(8,128)(2,1)S(1)}, bf16[64,8,256]{2,1,0:T(8,128)(2,1)S(1)}, u32[]{:S(2)}, u32[]{:S(2)}) collective-permute-start(bf16[64,8,256]{2,1,0:T(8,128)(2,1)S(1)} %copy-done.19), channel_id=1, source_target_pairs={{0,2},{2,4},{4,6},{6,8},{8,10},{10,12},{12,14},{1,3},{3,5},{5,7},{... | collective-permute-start | bytes 786440 | tf_op jit(solution)/shard_map/ppermute | solution.py:389
  29.7 0.9 slice_select_fusion
  30.6 0.0 copy-done.5
  30.6 0.0 copy-done.2
  30.7 7.4 %collective-permute-done.left = bf16[64,8,256]{2,1,0:T(8,128)(2,1)S(1)} collective-permute-done((bf16[64,8,256]{2,1,0:T(8,128)(2,1)S(1)}, bf16[64,8,256]{2,1,0:T(8,128)(2,1)S(1)}, u32[]{:S(2)}, u32[]{:S(2)}) %collective-permute-start) | collective-permute-done | bytes 262176 | tf_op jit(solution)/shard_map/ppermute | solution.py:389
  38.0 0.1 collective-permute-start.2
  38.1 0.0 copy-done.11
  38.1 0.0 copy-done.13
  38.1 0.0 copy-done.14
  38.2 0.0 copy-done.15
  38.2 0.0 copy-done.16
  38.2 0.0 copy-done.17
  38.2 0.0 copy-done.18
  38.2 0.6 stack.31.small
  38.8 0.6 collective-permute-done.2.edges
  39.4 0.0 copy-done.6
  39.4 0.6 copy-done.8
  40.0 14.1 %conv_first.1 = (bf16[66,80,256]{2,1,0:T(8,128)(2,1)}, f32[16,2,256]{2,1,0:T(2,128)}, f32[64,128]{1,0:T(8,128)}) custom-call(f32[16,8,256]{2,1,0:T(8,128)} %copy-done.2, f32[8,256]{1,0:T(8,128)} %stack.31.small, bf16[64,64,256]{2,1,0:T(8,128)(2,1)} %bitcast.22, bf16[64,8,256]{2,1,0:T(8,128)(2,1)} %copy-done.6, bf16[64,8,256]{2,1,0:T(8,128)(2,1)} %copy-done.5, ...), custom_call_target="tpu_custom_call" | custom-call | tf_op jit(solution)/shard_map/conv_first/pallas_call | solution.py:407
  54.1 0.0 all-to-all-done.2.refs_2_
  54.1 0.0 copy-start.1
  54.1 1.6 %collective-permute-start.4 = (bf16[8,7,48,128]{3,2,1,0:T(8,128)(2,1)S(1)}, bf16[8,7,48,128]{3,2,1,0:T(8,128)(2,1)S(1)}, u32[]{:S(2)}, u32[]{:S(2)}) collective-permute-start(bf16[8,7,48,128]{3,2,1,0:T(8,128)(2,1)S(1)} %all-to-all-done.2.refs_2_), channel_id=1, source_target_pairs={{0,16},{16,0},{1,17},{17,1},{2,18},{18,2},{3,19},{19,3},{4,20},{20... | collective-permute-start | bytes 2064392 | tf_op jit(solution)/shard_map/ppermute | solution.py:350
  55.7 14.0 %all-to-all-start.1 = ((f32[16,2,256]{2,1,0:T(2,128)}), f32[16,2,256]{2,1,0:T(2,128)S(1)}, u32[]{:S(2)}, u32[]{:S(2)}) async-start(f32[16,2,256]{2,1,0:T(2,128)} %get-tuple-element.16), calls=%async_computation.1 | async-start | bytes 65536 | tf_op jit(solution)/shard_map/all_to_all | solution.py:325
  69.7 0.0 copy-done
  69.7 1.0 %fusion = f32[1,3,3,256]{3,0,2,1:T(1,128)S(1)} fusion(bf16[3,3,256,256]{3,2,1,0:T(8,128)(2,1)S(1)} %copy-done, f32[256,1,1,1]{0,1,3,2:T(1,128)S(1)} %bitcast.27), kind=kOutput, calls=%fused_computation.6 | convolution fusion | flops 7077888 | bytes 1189888 | tf_op jit(solution)/shard_map/ijco,o->ijc/dot_general | solution.py:428
  70.7 0.6 copy.21
  71.4 4.9 %all-to-all-done.1.stats = f32[16,2,256]{2,1,0:T(2,128)S(1)} async-done(((f32[16,2,256]{2,1,0:T(2,128)}), f32[16,2,256]{2,1,0:T(2,128)S(1)}, u32[]{:S(2)}, u32[]{:S(2)}) %all-to-all-start.1) | async-done | bytes 32800 | tf_op jit(solution)/shard_map/all_to_all | solution.py:325
  76.3 0.6 copy-done.7
  76.9 5.0 %mel.1 = (f32[64,64]{1,0:T(8,128)}, bf16[64,128]{1,0:T(8,128)(2,1)}) custom-call(f32[16,2,256]{2,1,0:T(2,128)} %copy-done.7, f32[8,256]{1,0:T(8,128)} %stack.31.small, bf16[66,80,256]{2,1,0:T(8,128)(2,1)} %get-tuple-element.17.source, f32[3,3,256]{2,1,0:T(4,128)} %bitcast.25, f32[64,128]{1,0:T(8,128)} %get-tuple-element.18.base, f32[64,64]{1,0:T(8,128)} %noisy.3, ...), custom_call_target="tpu_custom_call" | custom-call | tf_op jit(solution)/shard_map/mel/pallas_call | solution.py:429
  81.9 0.0 copy-done.1
  81.9 0.1 collective-permute-start.5
  82.0 0.0 collective-permute-done.4.refs_3_
  82.0 0.0 copy-start.3
  82.0 0.5 collective-permute-start.6
  82.5 0.1 collective-permute-start.3
  82.6 0.0 copy-done.10
  82.6 0.1 reshape.15
  82.7 0.7 reshape.16.refs_6_
  83.4 0.0 copy-done.12
  83.4 0.6 broadcast_in_dim.10.refs_7_
  84.0 1.3 %collective-permute-done.3.refs_1_ = bf16[64,128]{1,0:T(8,128)(2,1)S(1)} collective-permute-done((bf16[64,128]{1,0:T(8,128)(2,1)}, bf16[64,128]{1,0:T(8,128)(2,1)S(1)}, u32[]{:S(2)}, u32[]{:S(2)}) %collective-permute-start.3) | collective-permute-done | bytes 16416 | tf_op jit(solution)/shard_map/ppermute | solution.py:455
  85.2 0.0 collective-permute-done.5.refs_4_
  85.3 0.0 collective-permute-done.6.refs_5_
  85.3 0.0 copy-done.3
  85.3 0.6 copy-done.9
  85.8 0.3 copy-done.4
  86.1 9.9 %up.1 = bf16[384,256]{1,0:T(8,128)(2,1)} custom-call(bf16[64,128]{1,0:T(8,128)(2,1)} %get-tuple-element.20.refs_0_, bf16[64,128]{1,0:T(8,128)(2,1)} %copy-done.9, bf16[8,7,48,128]{3,2,1,0:T(8,128)(2,1)} %copy-done.1, bf16[8,7,48,128]{3,2,1,0:T(8,128)(2,1)} %copy-done.3, bf16[8,7,48,128]{3,2,1,0:T(8,128)(2,1)} %copy-done.4, ...), custom_call_target="tpu_custom_call" | custom-call | tf_op jit(solution)/shard_map/up/pallas_call | solution.py:464
  (14 shorter events, 0.0 us)
Async XLA Ops:
  0.6 69.1 %copy-start = (bf16[3,3,256,256]{3,2,1,0:T(8,128)(2,1)S(1)}, bf16[3,3,256,256]{3,2,1,0:T(8,128)(2,1)}, u32[]{:S(2)}) copy-start(bf16[3,3,256,256]{3,2,1,0:T(8,128)(2,1)} %param.23) | copy-start | bytes 3538948
  3.7 11.4 %collective-permute-start.1 = (bf16[64,8,256]{2,1,0:T(8,128)(2,1)}, bf16[64,8,256]{2,1,0:T(8,128)(2,1)S(1)}, u32[]{:S(2)}, u32[]{:S(2)}) collective-permute-start(bf16[64,8,256]{2,1,0:T(8,128)(2,1)} %get-tuple-element.15), channel_id=1, source_target_pairs={{2,0},{4,2},{6,4},{8,6},{10,8},{12,10},{14,12},{3,1},{5,3},{7,5},{... | collective-permute-start | bytes 786440 | tf_op jit(solution)/shard_map/ppermute | solution.py:390
  4.9 16.5 %all-to-all-start = ((f32[16,8,256]{2,1,0:T(8,128)}), f32[16,8,256]{2,1,0:T(8,128)S(1)}, u32[]{:S(2)}, u32[]{:S(2)}) async-start(f32[16,8,256]{2,1,0:T(8,128)} %get-tuple-element.13), calls=%async_computation | async-start | bytes 262144 | tf_op jit(solution)/shard_map/all_to_all | solution.py:325
  13.5 12.4 %copy-start.19 = (bf16[64,8,256]{2,1,0:T(8,128)(2,1)S(1)}, bf16[64,8,256]{2,1,0:T(8,128)(2,1)}, u32[]{:S(2)}) copy-start(bf16[64,8,256]{2,1,0:T(8,128)(2,1)} %get-tuple-element.14) | copy-start | bytes 786436
  14.5 23.7 %copy-start.11 = (f32[256]{0:T(256)S(1)}, f32[256]{0:T(256)}, u32[]{:S(2)}) copy-start(f32[256]{0:T(256)} %param.25) | copy-start | bytes 3076
  14.5 23.7 %copy-start.13 = (f32[256]{0:T(256)S(1)}, f32[256]{0:T(256)}, u32[]{:S(2)}) copy-start(f32[256]{0:T(256)} %param.18) | copy-start | bytes 3076
  14.5 23.7 %copy-start.14 = (f32[256]{0:T(256)S(1)}, f32[256]{0:T(256)}, u32[]{:S(2)}) copy-start(f32[256]{0:T(256)} %param.19) | copy-start | bytes 3076
  14.5 23.7 %copy-start.15 = (f32[256]{0:T(256)S(1)}, f32[256]{0:T(256)}, u32[]{:S(2)}) copy-start(f32[256]{0:T(256)} %param.17) | copy-start | bytes 3076
  14.5 23.7 %copy-start.16 = (f32[256]{0:T(256)S(1)}, f32[256]{0:T(256)}, u32[]{:S(2)}) copy-start(f32[256]{0:T(256)} %param.21) | copy-start | bytes 3076
  14.5 23.7 %copy-start.17 = (f32[256]{0:T(256)S(1)}, f32[256]{0:T(256)}, u32[]{:S(2)}) copy-start(f32[256]{0:T(256)} %param.22) | copy-start | bytes 3076
  14.5 23.7 %copy-start.18 = (f32[256]{0:T(256)S(1)}, f32[256]{0:T(256)}, u32[]{:S(2)}) copy-start(f32[256]{0:T(256)} %param.24) | copy-start | bytes 3076
  15.1 15.6 %copy-start.5 = (bf16[64,8,256]{2,1,0:T(8,128)(2,1)}, bf16[64,8,256]{2,1,0:T(8,128)(2,1)S(1)}, u32[]{:S(2)}) copy-start(bf16[64,8,256]{2,1,0:T(8,128)(2,1)S(1)} %collective-permute-done.1.right) | copy-start | bytes 786436
  21.4 9.2 %copy-start.2 = (f32[16,8,256]{2,1,0:T(8,128)}, f32[16,8,256]{2,1,0:T(8,128)S(1)}, u32[]{:S(2)}) copy-start(f32[16,8,256]{2,1,0:T(8,128)S(1)} %all-to-all-done.stats.borders) | copy-start | bytes 393220
  22.3 31.7 %all-to-all-start.2 = ((bf16[8,7,48,128]{3,2,1,0:T(8,128)(2,1)}), bf16[8,7,48,128]{3,2,1,0:T(8,128)(2,1)S(1)}, u32[]{:S(2)}, u32[]{:S(2)}) async-start(bf16[8,7,48,128]{3,2,1,0:T(8,128)(2,1)} %broadcast_in_dim.4), calls=%async_computation.2 | async-start | bytes 1376256 | tf_op jit(solution)/shard_map/all_to_all | solution.py:348
  25.9 12.1 %collective-permute-start = (bf16[64,8,256]{2,1,0:T(8,128)(2,1)S(1)}, bf16[64,8,256]{2,1,0:T(8,128)(2,1)S(1)}, u32[]{:S(2)}, u32[]{:S(2)}) collective-permute-start(bf16[64,8,256]{2,1,0:T(8,128)(2,1)S(1)} %copy-done.19), channel_id=1, source_target_pairs={{0,2},{2,4},{4,6},{6,8},{8,10},{10,12},{12,14},{1,3},{3,5},{5,7},{... | collective-permute-start | bytes 786440 | tf_op jit(solution)/shard_map/ppermute | solution.py:389
  38.0 1.4 %copy-start.6 = (bf16[64,8,256]{2,1,0:T(8,128)(2,1)}, bf16[64,8,256]{2,1,0:T(8,128)(2,1)S(1)}, u32[]{:S(2)}) copy-start(bf16[64,8,256]{2,1,0:T(8,128)(2,1)S(1)} %collective-permute-done.left) | copy-start | bytes 786436
  38.0 1.3 %collective-permute-start.2 = (bf16[2,80,256]{2,1,0:T(8,128)(2,1)S(1)}, bf16[2,80,256]{2,1,0:T(8,128)(2,1)S(1)}, u32[]{:S(2)}, u32[]{:S(2)}) collective-permute-start(bf16[2,80,256]{2,1,0:T(8,128)(2,1)S(1)} %pad_maximum_fusion), channel_id=1, source_target_pairs={{0,1},{1,0},{2,3},{3,2},{4,5},{5,4},{6,7},{7,6},{8,9},{9,8},{10,11... | collective-permute-start | bytes 245768 | tf_op jit(solution)/shard_map/ppermute | solution.py:395
  39.4 0.6 copy-start.8
  54.1 27.8 %copy-start.1 = (bf16[8,7,48,128]{3,2,1,0:T(8,128)(2,1)}, bf16[8,7,48,128]{3,2,1,0:T(8,128)(2,1)S(1)}, u32[]{:S(2)}) copy-start(bf16[8,7,48,128]{3,2,1,0:T(8,128)(2,1)S(1)} %all-to-all-done.2.refs_2_) | copy-start | bytes 2064388
  54.1 27.9 %collective-permute-start.4 = (bf16[8,7,48,128]{3,2,1,0:T(8,128)(2,1)S(1)}, bf16[8,7,48,128]{3,2,1,0:T(8,128)(2,1)S(1)}, u32[]{:S(2)}, u32[]{:S(2)}) collective-permute-start(bf16[8,7,48,128]{3,2,1,0:T(8,128)(2,1)S(1)} %all-to-all-done.2.refs_2_), channel_id=1, source_target_pairs={{0,16},{16,0},{1,17},{17,1},{2,18},{18,2},{3,19},{19,3},{4,20},{20... | collective-permute-start | bytes 2064392 | tf_op jit(solution)/shard_map/ppermute | solution.py:350
  55.7 20.7 %all-to-all-start.1 = ((f32[16,2,256]{2,1,0:T(2,128)}), f32[16,2,256]{2,1,0:T(2,128)S(1)}, u32[]{:S(2)}, u32[]{:S(2)}) async-start(f32[16,2,256]{2,1,0:T(2,128)} %get-tuple-element.16), calls=%async_computation.1 | async-start | bytes 65536 | tf_op jit(solution)/shard_map/all_to_all | solution.py:325
  76.3 0.6 copy-start.7
  76.9 5.7 %copy-start.10 = (f32[1536]{0:T(1024)S(1)}, f32[1536]{0:T(1024)}, u32[]{:S(2)}) copy-start(f32[1536]{0:T(1024)} %param.27) | copy-start | bytes 18436
  76.9 6.4 %copy-start.12 = (f32[384]{0:T(512)S(1)}, f32[384]{0:T(512)}, u32[]{:S(2)}) copy-start(f32[384]{0:T(512)} %param.29) | copy-start | bytes 4612
  81.9 3.3 %collective-permute-start.5 = (bf16[8,7,48,128]{3,2,1,0:T(8,128)(2,1)S(1)}, bf16[8,7,48,128]{3,2,1,0:T(8,128)(2,1)S(1)}, u32[]{:S(2)}, u32[]{:S(2)}) collective-permute-start(bf16[8,7,48,128]{3,2,1,0:T(8,128)(2,1)S(1)} %all-to-all-done.2.refs_2_), channel_id=1, source_target_pairs={{0,1},{1,0},{2,3},{3,2},{4,5},{5,4},{6,7},{7,6},{8,9},{9,8},{10,11... | collective-permute-start | bytes 2064392 | tf_op jit(solution)/shard_map/ppermute | solution.py:351
  82.0 3.3 %copy-start.3 = (bf16[8,7,48,128]{3,2,1,0:T(8,128)(2,1)}, bf16[8,7,48,128]{3,2,1,0:T(8,128)(2,1)S(1)}, u32[]{:S(2)}) copy-start(bf16[8,7,48,128]{3,2,1,0:T(8,128)(2,1)S(1)} %collective-permute-done.4.refs_3_) | copy-start | bytes 2064388
  82.0 3.2 %collective-permute-start.6 = (bf16[8,7,48,128]{3,2,1,0:T(8,128)(2,1)S(1)}, bf16[8,7,48,128]{3,2,1,0:T(8,128)(2,1)}, u32[]{:S(2)}, u32[]{:S(2)}) collective-permute-start(bf16[8,7,48,128]{3,2,1,0:T(8,128)(2,1)S(1)} %collective-permute-done.4.refs_3_), channel_id=1, source_target_pairs={{0,1},{1,0},{2,3},{3,2},{4,5},{5,4},{6,7},{7,6},{8,9},{9,8},{10,11... | collective-permute-start | bytes 2064392 | tf_op jit(solution)/shard_map/ppermute | solution.py:352
  82.5 2.7 %collective-permute-start.3 = (bf16[64,128]{1,0:T(8,128)(2,1)}, bf16[64,128]{1,0:T(8,128)(2,1)S(1)}, u32[]{:S(2)}, u32[]{:S(2)}) collective-permute-start(bf16[64,128]{1,0:T(8,128)(2,1)} %get-tuple-element.20.refs_0_), channel_id=1, source_target_pairs={{0,1},{1,0},{2,3},{3,2},{4,5},{5,4},{6,7},{7,6},{8,9},{9,8},{10,11... | collective-permute-start | bytes 49160 | tf_op jit(solution)/shard_map/ppermute | solution.py:455
  85.2 0.6 copy-start.9
  85.2 0.9 copy-start.4
